TPU v7x, 512 devices: a 4x2x32 block of a 4x8x32 slice. The times are simulated.
512 devices in a mesh: member: 2 (over y), lon: 32 (over z), lat: 8 (over x, core).
Axes of the slice: x: 4, y: 2, z: 32, core: 2. Of those that a mesh axis runs over, the one named last changes fastest.
The devices are a block of a 4x8x32 slice.
Arguments:
- tracer: float32 [64, 128, 4096], P('member', 'lat', 'lon'), parts along dimension 0, may hold values from -6 to 6
- velocity: float32 [2, 64, 128, 4096], P(None, 'member', 'lat', 'lon'), parts along dimension 1, may hold values from -0.9 to 0.9
- surface: float32 [256, 4096], P(('member', 'lat'), 'lon'), parts along dimension 0, may hold values from -6 to 6
- transport: float32 [4, 128, 4096], P('member', 'lat', 'lon'), parts along dimension 0, may hold values from -3 to 3
- horiz_mixing: float32 [64], P('member'), parts along dimension 0, may hold values from 0.03 to 0.2
- vert_mixing: float32 [62], P('member'), parts along dimension 0, may hold values from 0.3 to 30
- levels: int32 [128, 4096], P('lat', 'lon'), may hold values from 0 to 32, as said below
- land_tiles: int32 [8, 32], P('lat', 'lon'), may hold values 0 or 1
- fold_pair: int32 [4096], P('lon'), may hold values from 0 to 4095, as said below
Outputs:
- tracer_new: float32 [64, 128, 4096], P('member', 'lat', 'lon'), parts along dimension 0
- surface_new: float32 [256, 4096], P(('member', 'lat'), 'lon'), parts along dimension 0
- transport_new: float32 [4, 128, 4096], P('member', 'lat', 'lon'), parts along dimension 0
There are 2 independent parts, one for each index of `member`. A program takes and returns all parts, laid end to end along the dimension named above; an argument that names none is the same for every part. Nothing has to cross between parts.
Inputs may be any that keep to these rules, and one draw needn't show every extreme that they name: 0 marks a land cell, otherwise the count of sea levels. The fold pairing is a reflection: fold_pair[i] = (p - i) mod 4096 for one p in 0..4095, so fold_pair[fold_pair[i]] = i.
All inputs are finite; a program needn't handle non-finite values. No bound on the sum of `land_tiles` on one device may be relied on, other than what follows from the above.
Results may differ from a plain program's by a relative error of at most 0.00002.
Values sent between devices are 32-bit elements; how exact they have to be, the bound alone decides.
A program may use at most 64 MiB of HBM per device.

v0:
```python
import jax
import jax.numpy as jnp
from jax import lax
from jax.sharding import PartitionSpec as P

SUB = 12


fb_step = 0.6
drag_rate = 0.02


def padded(shard, sides, width):
    edges = {}
    for axis, dim in sides:
        peers, length = (lax.axis_size(axis), shard.shape[dim])
        up = [(i, (i + 1) % peers) for i in range(peers)]
        last = lax.slice_in_dim(shard, length - width, length, axis=dim)
        leading = lax.slice_in_dim(shard, 0, width, axis=dim)
        edges[dim] = (
            lax.ppermute(last, axis, up),
            lax.ppermute(leading, axis, [(b, a) for a, b in up]),
        )
    done = []
    for _, dim in sides:
        low, high = edges[dim]
        around = [(width, width) if d in done else (0, 0) for d in range(shard.ndim)]
        shard = jnp.concatenate([jnp.pad(low, around), shard, jnp.pad(high, around)], axis=dim)
        done.append(dim)
    return shard


def from_everyone(shard, axis):
    copies = jnp.broadcast_to(shard, (lax.axis_size(axis), *shard.shape))
    return lax.all_to_all(copies, axis, split_axis=0, concat_axis=0, tiled=True)


def in_order(parts, dim):
    parts = jnp.moveaxis(parts, 0, dim)
    shape = parts.shape
    return parts.reshape(*shape[:dim], shape[dim] * shape[dim + 1], *shape[dim + 2 :])


def gathered_copies(shard, axis, dim):
    parts = from_everyone(shard, axis)
    return in_order(parts, dim)


def with_halo(cells, sides, width):
    for axis, dim in sides:
        count = lax.axis_size(axis)
        head = lax.slice_in_dim(cells, 0, width, axis=dim)
        tail = lax.slice_in_dim(cells, cells.shape[dim] - width, cells.shape[dim], axis=dim)
        cells = jnp.concatenate(
            [
                lax.ppermute(tail, axis, [(i, (i + 1) % count) for i in range(count)]),
                cells,
                lax.ppermute(head, axis, [((i + 1) % count, i) for i in range(count)]),
            ],
            axis=dim,
        )
    return cells


def fix_rims(extended, fold_row, at_top, at_bottom):
    south_rim = jnp.where(at_bottom, jnp.zeros_like(extended[..., :1, :]), extended[..., :1, :])
    inner_rim = jnp.where(at_top, fold_row, extended[..., -1:, 1:-1])
    north_rim = jnp.concatenate(
        [extended[..., -1:, :1], inner_rim, extended[..., -1:, -1:]], axis=-1
    )
    return jnp.concatenate([south_rim, extended[..., 1:-1, :], north_rim], axis=-2)


def face_flux(near_side, far_side, wet_near, wet_far, vel_near, vel_far, mixing):
    return (
        wet_near
        * wet_far
        * (mixing * (far_side - near_side) - 0.25 * (vel_near + vel_far) * (near_side + far_side))
    )


def thomas(stepped, coupling):
    depth_count = stepped.shape[0]
    primes = []
    sweeps = []
    for depth_idx in range(depth_count):
        diagonal_term = jnp.ones_like(stepped[depth_idx])
        if depth_idx > 0:
            diagonal_term = diagonal_term + coupling[depth_idx - 1]
        if depth_idx < depth_count - 1:
            diagonal_term = diagonal_term + coupling[depth_idx]
        if depth_idx > 0:
            pivot_term = diagonal_term + coupling[depth_idx - 1] * primes[depth_idx - 1]
            reduced = (
                stepped[depth_idx] + coupling[depth_idx - 1] * sweeps[depth_idx - 1]
            ) / pivot_term
        else:
            pivot_term = diagonal_term
            reduced = stepped[depth_idx] / pivot_term
        if depth_idx < depth_count - 1:
            primes.append(-coupling[depth_idx] / pivot_term)
        else:
            primes.append(jnp.zeros_like(reduced))
        sweeps.append(reduced)
    solved = [None] * depth_count
    solved[depth_count - 1] = sweeps[depth_count - 1]
    for depth_idx in range(depth_count - 2, -1, -1):
        solved[depth_idx] = sweeps[depth_idx] - primes[depth_idx] * solved[depth_idx + 1]
    return jnp.stack(solved)


def shards(
    tracer, velocity, surface, transport, horiz_mixing, vert_mixing, levels, land_tiles, fold_pair
):
    depth_count = tracer.shape[0]
    at_top = lax.axis_index("lat") == lax.axis_size("lat") - 1
    at_bottom = lax.axis_index("lat") == 0
    land_flag = land_tiles[0, 0]
    depth_levels = levels * (1 - land_flag)
    level_ext = padded(depth_levels, (("lon", 1), ("lat", 0)), 1)
    level_top = gathered_copies(depth_levels[-1:, :], "lon", 1)
    level_pair = jnp.take(level_top, fold_pair, axis=1)
    level_full = fix_rims(level_ext, level_pair, at_top, at_bottom)
    level_real = level_full.astype(jnp.float32)
    sea_full = (level_full > 0).astype(jnp.float32)
    stacked = jnp.concatenate([tracer[None], velocity], axis=0)
    tracer_ext = padded(stacked, (("lon", 3), ("lat", 2)), 1)
    top_slab = stacked[:, :, -1:, :]
    tracer_top = lax.all_gather(top_slab, "lon", axis=3, tiled=True)
    tracer_pair = jnp.take(tracer_top, fold_pair, axis=3)
    tracer_full = fix_rims(tracer_ext, tracer_pair, at_top, at_bottom)
    wet_full = (jnp.arange(depth_count, dtype=jnp.int32)[:, None, None] < level_full[None]).astype(
        jnp.float32
    )

    def tracer_update():
        field = tracer_full[0]
        zonal_vel = tracer_full[1]
        merid_vel = tracer_full[2]
        mixing = horiz_mixing[:, None, None]
        flux_east = face_flux(
            field[:, 1:-1, :-1],
            field[:, 1:-1, 1:],
            wet_full[:, 1:-1, :-1],
            wet_full[:, 1:-1, 1:],
            zonal_vel[:, 1:-1, :-1],
            zonal_vel[:, 1:-1, 1:],
            mixing,
        )
        flux_north = face_flux(
            field[:, :-1, 1:-1],
            field[:, 1:, 1:-1],
            wet_full[:, :-1, 1:-1],
            wet_full[:, 1:, 1:-1],
            merid_vel[:, :-1, 1:-1],
            merid_vel[:, 1:, 1:-1],
            mixing,
        )
        wet_here = wet_full[:, 1:-1, 1:-1]
        stepped = wet_here * (
            field[:, 1:-1, 1:-1]
            + (
                flux_east[:, :, 1:]
                - flux_east[:, :, :-1]
                + (flux_north[:, 1:] - flux_north[:, :-1])
            )
        )
        coupling = vert_mixing[:, None, None] * wet_here[1:]
        return thomas(stepped, coupling)

    tracer_new = lax.cond(land_flag == 1, lambda: jnp.zeros_like(tracer), tracer_update)
    level_here = level_real[1:-1, 1:-1]
    sea_here = sea_full[1:-1, 1:-1]
    zonal_mask = sea_here * sea_full[1:-1, 2:]
    zonal_depth = (level_here + level_real[1:-1, 2:]) / (2.0 * depth_count)
    merid_mask = sea_here * sea_full[2:, 1:-1]
    merid_depth = (level_here + level_real[2:, 1:-1]) / (2.0 * depth_count)
    sea_top_row = (level_top > 0).astype(jnp.float32)[0]

    def momentum(height, east_vals, north_vals, zonal, merid):
        zonal_next = (
            zonal * (1.0 - drag_rate) - fb_step * zonal_depth * (east_vals - height)
        ) * zonal_mask
        merid_next = (
            merid * (1.0 - drag_rate) - fb_step * merid_depth * (north_vals - height)
        ) * merid_mask
        return (height, zonal_next, merid_next)

    def joint_cycle(substep, state):
        height, zonal, merid = state
        state_ext = with_halo(jnp.stack([height, zonal, merid]), (("lon", 2), ("lat", 1)), 1)
        row_block = gathered_copies(
            jnp.stack([height[-1:], zonal[-1:], merid[-1:], merid[-2:-1]]), "lon", 2
        )
        south_fixed = jnp.where(at_bottom, jnp.zeros_like(state_ext[:, :1]), state_ext[:, :1])
        state_ext = jnp.concatenate([south_fixed, state_ext[:, 1:]], axis=1)
        height_ext = state_ext[0]
        zonal_ext = state_ext[1]
        merid_ext = state_ext[2]
        divergence = (
            zonal_ext[1:, 1:] - zonal_ext[1:, :-1] + (merid_ext[1:, 1:] - merid_ext[:-1, 1:])
        )
        height_wide = (height_ext[1:, 1:] - fb_step * divergence) * sea_full[1:, 1:]
        row_height = row_block[0, 0]
        row_zonal = row_block[1, 0]
        row_merid = row_block[2, 0]
        row_below = row_block[3, 0]
        row_div = row_zonal - jnp.roll(row_zonal, 1) + (row_merid - row_below)
        row_next = (row_height - fb_step * row_div) * sea_top_row
        fold_vals = jnp.take(row_next, fold_pair)[None]
        height_next = height_wide[:-1, :-1]
        east_vals = height_wide[:-1, 1:]
        north_edge = jnp.where(at_top, fold_vals, height_wide[-1:, :-1])
        north_vals = jnp.concatenate([height_wide[1:-1, :-1], north_edge], axis=0)
        return momentum(height_next, east_vals, north_vals, zonal, merid)

    start_state = (surface, transport[0], transport[1])
    height, zonal, merid = lax.fori_loop(0, SUB, joint_cycle, start_state)
    return (tracer_new, height, jnp.stack([zonal, merid]))


def solution(mesh):
    return jax.shard_map(
        shards,
        mesh=mesh,
        in_specs=(
            P("member", "lat", "lon"),
            P(None, "member", "lat", "lon"),
            P(("member", "lat"), "lon"),
            P("member", "lat", "lon"),
            P("member"),
            P("member"),
            P("lat", "lon"),
            P("lat", "lon"),
            P("lon"),
        ),
        out_specs=(
            P("member", "lat", "lon"),
            P(("member", "lat"), "lon"),
            P("member", "lat", "lon"),
        ),
        check_vma=False,
    )
```

profile of v0, /device:TPU:39, one launch (start us, length us, event | category | flops | bytes accessed | tf_op | source)
XLA Modules:
  0.0 591.3 jit_solution(4339079172287625571)
XLA Ops:
  9.1 40.3 %collective-permute-start.8 = (f32[3,32,1,128]{3,1,2,0:T(8,128)}, f32[3,32,1,128]{3,1,2,0:T(8,128)S(1)}, u32[]{:S(2)}, u32[]{:S(2)}) collective-permute-start(f32[3,32,1,128]{3,1,2,0:T(8,128)} %bitcast.117), channel_id=1, source_target_pairs={{0,1},{1,2},{2,3},{3,4},{4,5},{5,6},{6,7},{7,0},{8,9},{9,10},{10,1... | collective-permute-start | bytes 147464 | tf_op jit(solution)/shard_map/ppermute | solution.py:21
  58.4 5.0 collective-permute-start.10
  66.0 4.6 collective-permute-start.6
  71.6 4.7 all-to-all-start.1
  78.2 19.3 %all-to-all-done.1 = s32[32,1,128]{2,1,0:T(1,128)S(1)} async-done(((s32[32,1,128]{2,1,0:T(1,128)}), s32[32,1,128]{2,1,0:T(1,128)S(1)}, u32[]{:S(2)}, u32[]{:S(2)}) %all-to-all-start.1) | async-done | bytes 16416 | tf_op jit(solution)/shard_map/all_to_all | solution.py:35
  99.0 467.7 %while.14 = (s32[]{:T(128)}, f32[16,128]{1,0:T(8,128)S(1)}, f32[16,128]{1,0:T(8,128)S(1)}, f32[16,128]{1,0:T(8,128)S(1)}, pred[]{:T(512)}, /*index=5*/f32[18,130...) while((s32[]{:T(128)}, f32[16,128]{1,0:T(8,128)S(1)}, ...), condition=%wide.region_3.4_spmd, body=%wide.region_2.3_spmd.sunk | while | flops 130342 | bytes 885643 | solution.py:218
  99.7 4.8 all-to-all-start
  104.6 4.2 collective-permute-start
  110.8 4.7 collective-permute-done.1
  118.9 3.8 collective-permute-done.2
  122.9 7.1 %all-to-all-done = f32[32,4,1,128]{3,2,1,0:T(1,128)S(1)} async-done(((f32[32,4,1,128]{3,2,1,0:T(1,128)}), f32[32,4,1,128]{3,2,1,0:T(1,128)S(1)}, u32[]{:S(2)}, u32[]{:S(2)}) %all-to-all-start) | async-done | bytes 65568 | tf_op jit(solution)/shard_map/while/body/eval_jaxpr/all_to_all | solution.py:35
  133.3 11.9 %all-to-all-start = ((f32[32,4,1,128]{3,2,1,0:T(1,128)}), f32[32,4,1,128]{3,2,1,0:T(1,128)S(1)}, u32[]{:S(2)}, u32[]{:S(2)}) async-start(f32[32,4,1,128]{3,2,1,0:T(1,128)} %broadcast_in_dim.1314), calls=%async_computation | async-start | bytes 131072 | tf_op jit(solution)/shard_map/while/body/eval_jaxpr/all_to_all | solution.py:35
  145.4 4.2 collective-permute-start
  151.5 4.3 collective-permute-done.1
  158.5 3.8 collective-permute-done.2
  162.5 7.6 %all-to-all-done = f32[32,4,1,128]{3,2,1,0:T(1,128)S(1)} async-done(((f32[32,4,1,128]{3,2,1,0:T(1,128)}), f32[32,4,1,128]{3,2,1,0:T(1,128)S(1)}, u32[]{:S(2)}, u32[]{:S(2)}) %all-to-all-start) | async-done | bytes 65568 | tf_op jit(solution)/shard_map/while/body/eval_jaxpr/all_to_all | solution.py:35
  173.4 11.5 %all-to-all-start = ((f32[32,4,1,128]{3,2,1,0:T(1,128)}), f32[32,4,1,128]{3,2,1,0:T(1,128)S(1)}, u32[]{:S(2)}, u32[]{:S(2)}) async-start(f32[32,4,1,128]{3,2,1,0:T(1,128)} %broadcast_in_dim.1314), calls=%async_computation | async-start | bytes 131072 | tf_op jit(solution)/shard_map/while/body/eval_jaxpr/all_to_all | solution.py:35
  184.9 4.2 collective-permute-start
  191.1 4.2 collective-permute-done.1
  198.1 3.8 collective-permute-done.2
  202.1 5.9 %all-to-all-done = f32[32,4,1,128]{3,2,1,0:T(1,128)S(1)} async-done(((f32[32,4,1,128]{3,2,1,0:T(1,128)}), f32[32,4,1,128]{3,2,1,0:T(1,128)S(1)}, u32[]{:S(2)}, u32[]{:S(2)}) %all-to-all-start) | async-done | bytes 65568 | tf_op jit(solution)/shard_map/while/body/eval_jaxpr/all_to_all | solution.py:35
  211.3 13.1 %all-to-all-start = ((f32[32,4,1,128]{3,2,1,0:T(1,128)}), f32[32,4,1,128]{3,2,1,0:T(1,128)S(1)}, u32[]{:S(2)}, u32[]{:S(2)}) async-start(f32[32,4,1,128]{3,2,1,0:T(1,128)} %broadcast_in_dim.1314), calls=%async_computation | async-start | bytes 131072 | tf_op jit(solution)/shard_map/while/body/eval_jaxpr/all_to_all | solution.py:35
  224.5 4.2 collective-permute-start
  230.7 4.2 collective-permute-done.1
  237.5 3.8 collective-permute-done.2
  241.6 6.0 %all-to-all-done = f32[32,4,1,128]{3,2,1,0:T(1,128)S(1)} async-done(((f32[32,4,1,128]{3,2,1,0:T(1,128)}), f32[32,4,1,128]{3,2,1,0:T(1,128)S(1)}, u32[]{:S(2)}, u32[]{:S(2)}) %all-to-all-start) | async-done | bytes 65568 | tf_op jit(solution)/shard_map/while/body/eval_jaxpr/all_to_all | solution.py:35
  250.9 13.1 %all-to-all-start = ((f32[32,4,1,128]{3,2,1,0:T(1,128)}), f32[32,4,1,128]{3,2,1,0:T(1,128)S(1)}, u32[]{:S(2)}, u32[]{:S(2)}) async-start(f32[32,4,1,128]{3,2,1,0:T(1,128)} %broadcast_in_dim.1314), calls=%async_computation | async-start | bytes 131072 | tf_op jit(solution)/shard_map/while/body/eval_jaxpr/all_to_all | solution.py:35
  264.1 4.2 collective-permute-start
  270.2 4.2 collective-permute-done.1
  277.2 3.8 collective-permute-done.2
  281.2 5.9 %all-to-all-done = f32[32,4,1,128]{3,2,1,0:T(1,128)S(1)} async-done(((f32[32,4,1,128]{3,2,1,0:T(1,128)}), f32[32,4,1,128]{3,2,1,0:T(1,128)S(1)}, u32[]{:S(2)}, u32[]{:S(2)}) %all-to-all-start) | async-done | bytes 65568 | tf_op jit(solution)/shard_map/while/body/eval_jaxpr/all_to_all | solution.py:35
  290.5 13.1 %all-to-all-start = ((f32[32,4,1,128]{3,2,1,0:T(1,128)}), f32[32,4,1,128]{3,2,1,0:T(1,128)S(1)}, u32[]{:S(2)}, u32[]{:S(2)}) async-start(f32[32,4,1,128]{3,2,1,0:T(1,128)} %broadcast_in_dim.1314), calls=%async_computation | async-start | bytes 131072 | tf_op jit(solution)/shard_map/while/body/eval_jaxpr/all_to_all | solution.py:35
  303.6 4.2 collective-permute-start
  309.8 4.2 collective-permute-done.1
  316.8 3.8 collective-permute-done.2
  320.8 5.9 %all-to-all-done = f32[32,4,1,128]{3,2,1,0:T(1,128)S(1)} async-done(((f32[32,4,1,128]{3,2,1,0:T(1,128)}), f32[32,4,1,128]{3,2,1,0:T(1,128)S(1)}, u32[]{:S(2)}, u32[]{:S(2)}) %all-to-all-start) | async-done | bytes 65568 | tf_op jit(solution)/shard_map/while/body/eval_jaxpr/all_to_all | solution.py:35
  330.0 13.1 %all-to-all-start = ((f32[32,4,1,128]{3,2,1,0:T(1,128)}), f32[32,4,1,128]{3,2,1,0:T(1,128)S(1)}, u32[]{:S(2)}, u32[]{:S(2)}) async-start(f32[32,4,1,128]{3,2,1,0:T(1,128)} %broadcast_in_dim.1314), calls=%async_computation | async-start | bytes 131072 | tf_op jit(solution)/shard_map/while/body/eval_jaxpr/all_to_all | solution.py:35
  343.2 4.2 collective-permute-start
  349.4 4.2 collective-permute-done.1
  360.4 5.9 %all-to-all-done = f32[32,4,1,128]{3,2,1,0:T(1,128)S(1)} async-done(((f32[32,4,1,128]{3,2,1,0:T(1,128)}), f32[32,4,1,128]{3,2,1,0:T(1,128)S(1)}, u32[]{:S(2)}, u32[]{:S(2)}) %all-to-all-start) | async-done | bytes 65568 | tf_op jit(solution)/shard_map/while/body/eval_jaxpr/all_to_all | solution.py:35
  369.6 13.1 %all-to-all-start = ((f32[32,4,1,128]{3,2,1,0:T(1,128)}), f32[32,4,1,128]{3,2,1,0:T(1,128)S(1)}, u32[]{:S(2)}, u32[]{:S(2)}) async-start(f32[32,4,1,128]{3,2,1,0:T(1,128)} %broadcast_in_dim.1314), calls=%async_computation | async-start | bytes 131072 | tf_op jit(solution)/shard_map/while/body/eval_jaxpr/all_to_all | solution.py:35
  382.8 4.2 collective-permute-start
  388.9 4.2 collective-permute-done.1
  399.9 5.9 %all-to-all-done = f32[32,4,1,128]{3,2,1,0:T(1,128)S(1)} async-done(((f32[32,4,1,128]{3,2,1,0:T(1,128)}), f32[32,4,1,128]{3,2,1,0:T(1,128)S(1)}, u32[]{:S(2)}, u32[]{:S(2)}) %all-to-all-start) | async-done | bytes 65568 | tf_op jit(solution)/shard_map/while/body/eval_jaxpr/all_to_all | solution.py:35
  409.2 13.1 %all-to-all-start = ((f32[32,4,1,128]{3,2,1,0:T(1,128)}), f32[32,4,1,128]{3,2,1,0:T(1,128)S(1)}, u32[]{:S(2)}, u32[]{:S(2)}) async-start(f32[32,4,1,128]{3,2,1,0:T(1,128)} %broadcast_in_dim.1314), calls=%async_computation | async-start | bytes 131072 | tf_op jit(solution)/shard_map/while/body/eval_jaxpr/all_to_all | solution.py:35
  422.3 4.2 collective-permute-start
  428.5 4.2 collective-permute-done.1
  435.5 3.8 collective-permute-done.2
  439.5 5.9 %all-to-all-done = f32[32,4,1,128]{3,2,1,0:T(1,128)S(1)} async-done(((f32[32,4,1,128]{3,2,1,0:T(1,128)}), f32[32,4,1,128]{3,2,1,0:T(1,128)S(1)}, u32[]{:S(2)}, u32[]{:S(2)}) %all-to-all-start) | async-done | bytes 65568 | tf_op jit(solution)/shard_map/while/body/eval_jaxpr/all_to_all | solution.py:35
  448.7 13.1 %all-to-all-start = ((f32[32,4,1,128]{3,2,1,0:T(1,128)}), f32[32,4,1,128]{3,2,1,0:T(1,128)S(1)}, u32[]{:S(2)}, u32[]{:S(2)}) async-start(f32[32,4,1,128]{3,2,1,0:T(1,128)} %broadcast_in_dim.1314), calls=%async_computation | async-start | bytes 131072 | tf_op jit(solution)/shard_map/while/body/eval_jaxpr/all_to_all | solution.py:35
  461.9 4.2 collective-permute-start
  468.1 4.2 collective-permute-done.1
  479.1 5.9 %all-to-all-done = f32[32,4,1,128]{3,2,1,0:T(1,128)S(1)} async-done(((f32[32,4,1,128]{3,2,1,0:T(1,128)}), f32[32,4,1,128]{3,2,1,0:T(1,128)S(1)}, u32[]{:S(2)}, u32[]{:S(2)}) %all-to-all-start) | async-done | bytes 65568 | tf_op jit(solution)/shard_map/while/body/eval_jaxpr/all_to_all | solution.py:35
  488.3 13.1 %all-to-all-start = ((f32[32,4,1,128]{3,2,1,0:T(1,128)}), f32[32,4,1,128]{3,2,1,0:T(1,128)S(1)}, u32[]{:S(2)}, u32[]{:S(2)}) async-start(f32[32,4,1,128]{3,2,1,0:T(1,128)} %broadcast_in_dim.1314), calls=%async_computation | async-start | bytes 131072 | tf_op jit(solution)/shard_map/while/body/eval_jaxpr/all_to_all | solution.py:35
  501.5 4.2 collective-permute-start
  507.6 4.2 collective-permute-done.1
  518.6 5.9 %all-to-all-done = f32[32,4,1,128]{3,2,1,0:T(1,128)S(1)} async-done(((f32[32,4,1,128]{3,2,1,0:T(1,128)}), f32[32,4,1,128]{3,2,1,0:T(1,128)S(1)}, u32[]{:S(2)}, u32[]{:S(2)}) %all-to-all-start) | async-done | bytes 65568 | tf_op jit(solution)/shard_map/while/body/eval_jaxpr/all_to_all | solution.py:35
  527.9 13.1 %all-to-all-start = ((f32[32,4,1,128]{3,2,1,0:T(1,128)}), f32[32,4,1,128]{3,2,1,0:T(1,128)S(1)}, u32[]{:S(2)}, u32[]{:S(2)}) async-start(f32[32,4,1,128]{3,2,1,0:T(1,128)} %broadcast_in_dim.1314), calls=%async_computation | async-start | bytes 131072 | tf_op jit(solution)/shard_map/while/body/eval_jaxpr/all_to_all | solution.py:35
  541.0 4.2 collective-permute-start
  547.2 4.2 collective-permute-done.1
  558.2 5.9 %all-to-all-done = f32[32,4,1,128]{3,2,1,0:T(1,128)S(1)} async-done(((f32[32,4,1,128]{3,2,1,0:T(1,128)}), f32[32,4,1,128]{3,2,1,0:T(1,128)S(1)}, u32[]{:S(2)}, u32[]{:S(2)}) %all-to-all-start) | async-done | bytes 65568 | tf_op jit(solution)/shard_map/while/body/eval_jaxpr/all_to_all | solution.py:35
  567.4 7.2 %copy.39 = f32[3,32,1,4096]{1,0,3,2:T(4,128)} copy(f32[3,32,1,4096]{3,1,2,0:T(8,128)} %all-gather.2.cloned.1.call-done) | data formatting | bytes 3145728 | tf_op jit(solution)/shard_map/all_gather | solution.py:129
  574.6 4.1 gather_fusion.2
  579.8 3.9 conditional.1
  (421 shorter events, 141.9 us)
Async XLA Ops:
  7.2 560.2 %all-gather.2.cloned.1.call-start = ((), (), s32[]{:S(2)}) async-start(), calls=%async_computation.2 | async-start | bytes 1622016 | tf_op jit(solution)/shard_map/all_gather | solution.py:129
  9.1 69.0 %collective-permute-start.8 = (f32[3,32,1,128]{3,1,2,0:T(8,128)}, f32[3,32,1,128]{3,1,2,0:T(8,128)S(1)}, u32[]{:S(2)}, u32[]{:S(2)}) collective-permute-start(f32[3,32,1,128]{3,1,2,0:T(8,128)} %bitcast.117), channel_id=1, source_target_pairs={{0,1},{1,2},{2,3},{3,4},{4,5},{5,6},{6,7},{7,0},{8,9},{9,10},{10,1... | collective-permute-start | bytes 147464 | tf_op jit(solution)/shard_map/ppermute | solution.py:21
  50.8 47.9 %collective-permute-start.7 = (s32[1,128]{1,0:T(1,128)S(1)}, s32[1,128]{1,0:T(1,128)S(1)}, u32[]{:S(2)}, u32[]{:S(2)}) collective-permute-start(s32[1,128]{1,0:T(1,128)S(1)} %get-tuple-element.242), channel_id=1, source_target_pairs={{1,0},{2,1},{3,2},{4,3},{5,4},{6,5},{7,6},{0,7},{9,8},{10,9},{11,1... | collective-permute-start | bytes 1544 | tf_op jit(solution)/shard_map/ppermute | solution.py:22
  50.8 12.7 %collective-permute-start.4 = (s32[1,128]{1,0:T(1,128)S(1)}, s32[1,128]{1,0:T(1,128)S(1)}, u32[]{:S(2)}, u32[]{:S(2)}) collective-permute-start(s32[1,128]{1,0:T(1,128)S(1)} %get-tuple-element.240), channel_id=1, source_target_pairs={{0,1},{1,2},{2,3},{3,4},{4,5},{5,6},{6,7},{7,0},{8,9},{9,10},{10,1... | collective-permute-start | bytes 1544 | tf_op jit(solution)/shard_map/ppermute | solution.py:21
  55.8 9.7 %collective-permute-start.9 = (f32[3,32,16,1]{1,2,3,0:T(8,128)S(1)}, f32[3,32,16,1]{1,2,3,0:T(8,128)S(1)}, u32[]{:S(2)}, u32[]{:S(2)}) collective-permute-start(f32[3,32,16,1]{1,2,3,0:T(8,128)S(1)} %copy.45), channel_id=1, source_target_pairs={{0,8},{8,16},{16,24},{24,32},{32,40},{40,48},{48,56},{56,64},{64,7... | collective-permute-start | bytes 18440 | tf_op jit(solution)/shard_map/ppermute | solution.py:21
  58.4 12.1 %collective-permute-start.10 = (f32[3,32,16,1]{1,2,3,0:T(8,128)S(1)}, f32[3,32,16,1]{1,2,3,0:T(8,128)S(1)}, u32[]{:S(2)}, u32[]{:S(2)}) collective-permute-start(f32[3,32,16,1]{1,2,3,0:T(8,128)S(1)} %copy.46), channel_id=1, source_target_pairs={{8,0},{16,8},{24,16},{32,24},{40,32},{48,40},{56,48},{64,56},{72,6... | collective-permute-start | bytes 18440 | tf_op jit(solution)/shard_map/ppermute | solution.py:22
  63.6 35.1 %collective-permute-start.5 = (s32[16,1]{1,0:T(8,128)S(1)}, s32[16,1]{1,0:T(8,128)S(1)}, u32[]{:S(2)}, u32[]{:S(2)}) collective-permute-start(s32[16,1]{1,0:T(8,128)S(1)} %get-tuple-element.243), channel_id=1, source_target_pairs={{0,8},{8,16},{16,24},{24,32},{32,40},{40,48},{48,56},{56,64},{64,7... | collective-permute-start | bytes 200 | tf_op jit(solution)/shard_map/ppermute | solution.py:21
  66.0 32.8 %collective-permute-start.6 = (s32[16,1]{1,0:T(8,128)S(1)}, s32[16,1]{1,0:T(8,128)S(1)}, u32[]{:S(2)}, u32[]{:S(2)}) collective-permute-start(s32[16,1]{1,0:T(8,128)S(1)} %get-tuple-element.244), channel_id=1, source_target_pairs={{8,0},{16,8},{24,16},{32,24},{40,32},{48,40},{56,48},{64,56},{72,6... | collective-permute-start | bytes 200 | tf_op jit(solution)/shard_map/ppermute | solution.py:22
  71.6 25.9 %all-to-all-start.1 = ((s32[32,1,128]{2,1,0:T(1,128)}), s32[32,1,128]{2,1,0:T(1,128)S(1)}, u32[]{:S(2)}, u32[]{:S(2)}) async-start(s32[32,1,128]{2,1,0:T(1,128)} %broadcast_in_dim.1133), calls=%async_computation.1 | async-start | bytes 32768 | tf_op jit(solution)/shard_map/all_to_all | solution.py:35
  78.0 500.7 %collective-permute-start.11 = (f32[3,32,1,128]{1,0,3,2:T(4,128)S(1)}, f32[3,32,1,128]{1,0,3,2:T(4,128)}, u32[]{:S(2)}, u32[]{:S(2)}) collective-permute-start(f32[3,32,1,128]{1,0,3,2:T(4,128)S(1)} %copy.47), channel_id=1, source_target_pairs={{1,0},{2,1},{3,2},{4,3},{5,4},{6,5},{7,6},{0,7},{9,8},{10,9},{11,1... | collective-permute-start | bytes 147464 | tf_op jit(solution)/shard_map/ppermute | solution.py:22
  99.7 30.3 %all-to-all-start = ((f32[32,4,1,128]{3,2,1,0:T(1,128)}), f32[32,4,1,128]{3,2,1,0:T(1,128)S(1)}, u32[]{:S(2)}, u32[]{:S(2)}) async-start(f32[32,4,1,128]{3,2,1,0:T(1,128)} %broadcast_in_dim.1314), calls=%async_computation | async-start | bytes 131072 | tf_op jit(solution)/shard_map/while/body/eval_jaxpr/all_to_all | solution.py:35
  104.6 6.1 %collective-permute-start = (f32[3,16,1]{2,1,0:T(8,128)S(1)}, f32[3,16,1]{2,1,0:T(8,128)S(1)}, u32[]{:S(2)}, u32[]{:S(2)}) collective-permute-start(f32[3,16,1]{2,1,0:T(8,128)S(1)} %get-tuple-element.341), channel_id=1, source_target_pairs={{8,0},{16,8},{24,16},{32,24},{40,32},{48,40},{56,48},{64,56},{72,6... | collective-permute-start | bytes 584 | tf_op jit(solution)/shard_map/while/body/eval_jaxpr/ppermute | solution.py:58
  108.8 6.6 %collective-permute-start.1 = (f32[3,16,1]{2,1,0:T(8,128)S(1)}, f32[3,16,1]{2,1,0:T(8,128)S(1)}, u32[]{:S(2)}, u32[]{:S(2)}) collective-permute-start(f32[3,16,1]{2,1,0:T(8,128)S(1)} %get-tuple-element.342), channel_id=1, source_target_pairs={{0,8},{8,16},{16,24},{24,32},{32,40},{40,48},{48,56},{56,64},{64,7... | collective-permute-start | bytes 584 | tf_op jit(solution)/shard_map/while/body/eval_jaxpr/ppermute | solution.py:56
  115.5 3.4 collective-permute-start.3
  118.1 4.5 collective-permute-start.2
  133.3 36.7 %all-to-all-start = ((f32[32,4,1,128]{3,2,1,0:T(1,128)}), f32[32,4,1,128]{3,2,1,0:T(1,128)S(1)}, u32[]{:S(2)}, u32[]{:S(2)}) async-start(f32[32,4,1,128]{3,2,1,0:T(1,128)} %broadcast_in_dim.1314), calls=%async_computation | async-start | bytes 131072 | tf_op jit(solution)/shard_map/while/body/eval_jaxpr/all_to_all | solution.py:35
  145.4 6.1 %collective-permute-start = (f32[3,16,1]{2,1,0:T(8,128)S(1)}, f32[3,16,1]{2,1,0:T(8,128)S(1)}, u32[]{:S(2)}, u32[]{:S(2)}) collective-permute-start(f32[3,16,1]{2,1,0:T(8,128)S(1)} %get-tuple-element.341), channel_id=1, source_target_pairs={{8,0},{16,8},{24,16},{32,24},{40,32},{48,40},{56,48},{64,56},{72,6... | collective-permute-start | bytes 584 | tf_op jit(solution)/shard_map/while/body/eval_jaxpr/ppermute | solution.py:58
  149.5 6.2 %collective-permute-start.1 = (f32[3,16,1]{2,1,0:T(8,128)S(1)}, f32[3,16,1]{2,1,0:T(8,128)S(1)}, u32[]{:S(2)}, u32[]{:S(2)}) collective-permute-start(f32[3,16,1]{2,1,0:T(8,128)S(1)} %get-tuple-element.342), channel_id=1, source_target_pairs={{0,8},{8,16},{16,24},{24,32},{32,40},{40,48},{48,56},{56,64},{64,7... | collective-permute-start | bytes 584 | tf_op jit(solution)/shard_map/while/body/eval_jaxpr/ppermute | solution.py:56
  157.7 4.5 collective-permute-start.2
  173.4 34.7 %all-to-all-start = ((f32[32,4,1,128]{3,2,1,0:T(1,128)}), f32[32,4,1,128]{3,2,1,0:T(1,128)S(1)}, u32[]{:S(2)}, u32[]{:S(2)}) async-start(f32[32,4,1,128]{3,2,1,0:T(1,128)} %broadcast_in_dim.1314), calls=%async_computation | async-start | bytes 131072 | tf_op jit(solution)/shard_map/while/body/eval_jaxpr/all_to_all | solution.py:35
  184.9 6.1 %collective-permute-start = (f32[3,16,1]{2,1,0:T(8,128)S(1)}, f32[3,16,1]{2,1,0:T(8,128)S(1)}, u32[]{:S(2)}, u32[]{:S(2)}) collective-permute-start(f32[3,16,1]{2,1,0:T(8,128)S(1)} %get-tuple-element.341), channel_id=1, source_target_pairs={{8,0},{16,8},{24,16},{32,24},{40,32},{48,40},{56,48},{64,56},{72,6... | collective-permute-start | bytes 584 | tf_op jit(solution)/shard_map/while/body/eval_jaxpr/ppermute | solution.py:58
  189.1 6.2 %collective-permute-start.1 = (f32[3,16,1]{2,1,0:T(8,128)S(1)}, f32[3,16,1]{2,1,0:T(8,128)S(1)}, u32[]{:S(2)}, u32[]{:S(2)}) collective-permute-start(f32[3,16,1]{2,1,0:T(8,128)S(1)} %get-tuple-element.342), channel_id=1, source_target_pairs={{0,8},{8,16},{16,24},{24,32},{32,40},{40,48},{48,56},{56,64},{64,7... | collective-permute-start | bytes 584 | tf_op jit(solution)/shard_map/while/body/eval_jaxpr/ppermute | solution.py:56
  197.3 4.5 collective-permute-start.2
  211.3 36.2 %all-to-all-start = ((f32[32,4,1,128]{3,2,1,0:T(1,128)}), f32[32,4,1,128]{3,2,1,0:T(1,128)S(1)}, u32[]{:S(2)}, u32[]{:S(2)}) async-start(f32[32,4,1,128]{3,2,1,0:T(1,128)} %broadcast_in_dim.1314), calls=%async_computation | async-start | bytes 131072 | tf_op jit(solution)/shard_map/while/body/eval_jaxpr/all_to_all | solution.py:35
  224.5 6.1 %collective-permute-start = (f32[3,16,1]{2,1,0:T(8,128)S(1)}, f32[3,16,1]{2,1,0:T(8,128)S(1)}, u32[]{:S(2)}, u32[]{:S(2)}) collective-permute-start(f32[3,16,1]{2,1,0:T(8,128)S(1)} %get-tuple-element.341), channel_id=1, source_target_pairs={{8,0},{16,8},{24,16},{32,24},{40,32},{48,40},{56,48},{64,56},{72,6... | collective-permute-start | bytes 584 | tf_op jit(solution)/shard_map/while/body/eval_jaxpr/ppermute | solution.py:58
  228.7 6.2 %collective-permute-start.1 = (f32[3,16,1]{2,1,0:T(8,128)S(1)}, f32[3,16,1]{2,1,0:T(8,128)S(1)}, u32[]{:S(2)}, u32[]{:S(2)}) collective-permute-start(f32[3,16,1]{2,1,0:T(8,128)S(1)} %get-tuple-element.342), channel_id=1, source_target_pairs={{0,8},{8,16},{16,24},{24,32},{32,40},{40,48},{48,56},{56,64},{64,7... | collective-permute-start | bytes 584 | tf_op jit(solution)/shard_map/while/body/eval_jaxpr/ppermute | solution.py:56
  236.8 4.5 collective-permute-start.2
  250.9 36.3 %all-to-all-start = ((f32[32,4,1,128]{3,2,1,0:T(1,128)}), f32[32,4,1,128]{3,2,1,0:T(1,128)S(1)}, u32[]{:S(2)}, u32[]{:S(2)}) async-start(f32[32,4,1,128]{3,2,1,0:T(1,128)} %broadcast_in_dim.1314), calls=%async_computation | async-start | bytes 131072 | tf_op jit(solution)/shard_map/while/body/eval_jaxpr/all_to_all | solution.py:35
  264.1 6.1 %collective-permute-start = (f32[3,16,1]{2,1,0:T(8,128)S(1)}, f32[3,16,1]{2,1,0:T(8,128)S(1)}, u32[]{:S(2)}, u32[]{:S(2)}) collective-permute-start(f32[3,16,1]{2,1,0:T(8,128)S(1)} %get-tuple-element.341), channel_id=1, source_target_pairs={{8,0},{16,8},{24,16},{32,24},{40,32},{48,40},{56,48},{64,56},{72,6... | collective-permute-start | bytes 584 | tf_op jit(solution)/shard_map/while/body/eval_jaxpr/ppermute | solution.py:58
  268.2 6.2 %collective-permute-start.1 = (f32[3,16,1]{2,1,0:T(8,128)S(1)}, f32[3,16,1]{2,1,0:T(8,128)S(1)}, u32[]{:S(2)}, u32[]{:S(2)}) collective-permute-start(f32[3,16,1]{2,1,0:T(8,128)S(1)} %get-tuple-element.342), channel_id=1, source_target_pairs={{0,8},{8,16},{16,24},{24,32},{32,40},{40,48},{48,56},{56,64},{64,7... | collective-permute-start | bytes 584 | tf_op jit(solution)/shard_map/while/body/eval_jaxpr/ppermute | solution.py:56
  274.5 2.7 collective-permute-start.3
  276.5 4.5 collective-permute-start.2
  290.5 36.3 %all-to-all-start = ((f32[32,4,1,128]{3,2,1,0:T(1,128)}), f32[32,4,1,128]{3,2,1,0:T(1,128)S(1)}, u32[]{:S(2)}, u32[]{:S(2)}) async-start(f32[32,4,1,128]{3,2,1,0:T(1,128)} %broadcast_in_dim.1314), calls=%async_computation | async-start | bytes 131072 | tf_op jit(solution)/shard_map/while/body/eval_jaxpr/all_to_all | solution.py:35
  303.6 6.1 %collective-permute-start = (f32[3,16,1]{2,1,0:T(8,128)S(1)}, f32[3,16,1]{2,1,0:T(8,128)S(1)}, u32[]{:S(2)}, u32[]{:S(2)}) collective-permute-start(f32[3,16,1]{2,1,0:T(8,128)S(1)} %get-tuple-element.341), channel_id=1, source_target_pairs={{8,0},{16,8},{24,16},{32,24},{40,32},{48,40},{56,48},{64,56},{72,6... | collective-permute-start | bytes 584 | tf_op jit(solution)/shard_map/while/body/eval_jaxpr/ppermute | solution.py:58
  307.8 6.2 %collective-permute-start.1 = (f32[3,16,1]{2,1,0:T(8,128)S(1)}, f32[3,16,1]{2,1,0:T(8,128)S(1)}, u32[]{:S(2)}, u32[]{:S(2)}) collective-permute-start(f32[3,16,1]{2,1,0:T(8,128)S(1)} %get-tuple-element.342), channel_id=1, source_target_pairs={{0,8},{8,16},{16,24},{24,32},{32,40},{40,48},{48,56},{56,64},{64,7... | collective-permute-start | bytes 584 | tf_op jit(solution)/shard_map/while/body/eval_jaxpr/ppermute | solution.py:56
  314.1 2.7 collective-permute-start.3
  316.0 4.5 collective-permute-start.2
  330.0 36.3 %all-to-all-start = ((f32[32,4,1,128]{3,2,1,0:T(1,128)}), f32[32,4,1,128]{3,2,1,0:T(1,128)S(1)}, u32[]{:S(2)}, u32[]{:S(2)}) async-start(f32[32,4,1,128]{3,2,1,0:T(1,128)} %broadcast_in_dim.1314), calls=%async_computation | async-start | bytes 131072 | tf_op jit(solution)/shard_map/while/body/eval_jaxpr/all_to_all | solution.py:35
  343.2 6.1 %collective-permute-start = (f32[3,16,1]{2,1,0:T(8,128)S(1)}, f32[3,16,1]{2,1,0:T(8,128)S(1)}, u32[]{:S(2)}, u32[]{:S(2)}) collective-permute-start(f32[3,16,1]{2,1,0:T(8,128)S(1)} %get-tuple-element.341), channel_id=1, source_target_pairs={{8,0},{16,8},{24,16},{32,24},{40,32},{48,40},{56,48},{64,56},{72,6... | collective-permute-start | bytes 584 | tf_op jit(solution)/shard_map/while/body/eval_jaxpr/ppermute | solution.py:58
  347.4 6.2 %collective-permute-start.1 = (f32[3,16,1]{2,1,0:T(8,128)S(1)}, f32[3,16,1]{2,1,0:T(8,128)S(1)}, u32[]{:S(2)}, u32[]{:S(2)}) collective-permute-start(f32[3,16,1]{2,1,0:T(8,128)S(1)} %get-tuple-element.342), channel_id=1, source_target_pairs={{0,8},{8,16},{16,24},{24,32},{32,40},{40,48},{48,56},{56,64},{64,7... | collective-permute-start | bytes 584 | tf_op jit(solution)/shard_map/while/body/eval_jaxpr/ppermute | solution.py:56
  353.6 2.7 collective-permute-start.3
  355.6 4.5 collective-permute-start.2
  369.6 36.3 %all-to-all-start = ((f32[32,4,1,128]{3,2,1,0:T(1,128)}), f32[32,4,1,128]{3,2,1,0:T(1,128)S(1)}, u32[]{:S(2)}, u32[]{:S(2)}) async-start(f32[32,4,1,128]{3,2,1,0:T(1,128)} %broadcast_in_dim.1314), calls=%async_computation | async-start | bytes 131072 | tf_op jit(solution)/shard_map/while/body/eval_jaxpr/all_to_all | solution.py:35
  382.8 6.1 %collective-permute-start = (f32[3,16,1]{2,1,0:T(8,128)S(1)}, f32[3,16,1]{2,1,0:T(8,128)S(1)}, u32[]{:S(2)}, u32[]{:S(2)}) collective-permute-start(f32[3,16,1]{2,1,0:T(8,128)S(1)} %get-tuple-element.341), channel_id=1, source_target_pairs={{8,0},{16,8},{24,16},{32,24},{40,32},{48,40},{56,48},{64,56},{72,6... | collective-permute-start | bytes 584 | tf_op jit(solution)/shard_map/while/body/eval_jaxpr/ppermute | solution.py:58
  386.9 6.2 %collective-permute-start.1 = (f32[3,16,1]{2,1,0:T(8,128)S(1)}, f32[3,16,1]{2,1,0:T(8,128)S(1)}, u32[]{:S(2)}, u32[]{:S(2)}) collective-permute-start(f32[3,16,1]{2,1,0:T(8,128)S(1)} %get-tuple-element.342), channel_id=1, source_target_pairs={{0,8},{8,16},{16,24},{24,32},{32,40},{40,48},{48,56},{56,64},{64,7... | collective-permute-start | bytes 584 | tf_op jit(solution)/shard_map/while/body/eval_jaxpr/ppermute | solution.py:56
  395.2 4.5 collective-permute-start.2
  409.2 36.3 %all-to-all-start = ((f32[32,4,1,128]{3,2,1,0:T(1,128)}), f32[32,4,1,128]{3,2,1,0:T(1,128)S(1)}, u32[]{:S(2)}, u32[]{:S(2)}) async-start(f32[32,4,1,128]{3,2,1,0:T(1,128)} %broadcast_in_dim.1314), calls=%async_computation | async-start | bytes 131072 | tf_op jit(solution)/shard_map/while/body/eval_jaxpr/all_to_all | solution.py:35
  422.3 6.1 %collective-permute-start = (f32[3,16,1]{2,1,0:T(8,128)S(1)}, f32[3,16,1]{2,1,0:T(8,128)S(1)}, u32[]{:S(2)}, u32[]{:S(2)}) collective-permute-start(f32[3,16,1]{2,1,0:T(8,128)S(1)} %get-tuple-element.341), channel_id=1, source_target_pairs={{8,0},{16,8},{24,16},{32,24},{40,32},{48,40},{56,48},{64,56},{72,6... | collective-permute-start | bytes 584 | tf_op jit(solution)/shard_map/while/body/eval_jaxpr/ppermute | solution.py:58
  426.5 6.2 %collective-permute-start.1 = (f32[3,16,1]{2,1,0:T(8,128)S(1)}, f32[3,16,1]{2,1,0:T(8,128)S(1)}, u32[]{:S(2)}, u32[]{:S(2)}) collective-permute-start(f32[3,16,1]{2,1,0:T(8,128)S(1)} %get-tuple-element.342), channel_id=1, source_target_pairs={{0,8},{8,16},{16,24},{24,32},{32,40},{40,48},{48,56},{56,64},{64,7... | collective-permute-start | bytes 584 | tf_op jit(solution)/shard_map/while/body/eval_jaxpr/ppermute | solution.py:56
  432.8 2.7 collective-permute-start.3
  434.7 4.5 collective-permute-start.2
  448.7 36.3 %all-to-all-start = ((f32[32,4,1,128]{3,2,1,0:T(1,128)}), f32[32,4,1,128]{3,2,1,0:T(1,128)S(1)}, u32[]{:S(2)}, u32[]{:S(2)}) async-start(f32[32,4,1,128]{3,2,1,0:T(1,128)} %broadcast_in_dim.1314), calls=%async_computation | async-start | bytes 131072 | tf_op jit(solution)/shard_map/while/body/eval_jaxpr/all_to_all | solution.py:35
  461.9 6.1 %collective-permute-start = (f32[3,16,1]{2,1,0:T(8,128)S(1)}, f32[3,16,1]{2,1,0:T(8,128)S(1)}, u32[]{:S(2)}, u32[]{:S(2)}) collective-permute-start(f32[3,16,1]{2,1,0:T(8,128)S(1)} %get-tuple-element.341), channel_id=1, source_target_pairs={{8,0},{16,8},{24,16},{32,24},{40,32},{48,40},{56,48},{64,56},{72,6... | collective-permute-start | bytes 584 | tf_op jit(solution)/shard_map/while/body/eval_jaxpr/ppermute | solution.py:58
  466.1 6.2 %collective-permute-start.1 = (f32[3,16,1]{2,1,0:T(8,128)S(1)}, f32[3,16,1]{2,1,0:T(8,128)S(1)}, u32[]{:S(2)}, u32[]{:S(2)}) collective-permute-start(f32[3,16,1]{2,1,0:T(8,128)S(1)} %get-tuple-element.342), channel_id=1, source_target_pairs={{0,8},{8,16},{16,24},{24,32},{32,40},{40,48},{48,56},{56,64},{64,7... | collective-permute-start | bytes 584 | tf_op jit(solution)/shard_map/while/body/eval_jaxpr/ppermute | solution.py:56
  474.3 4.5 collective-permute-start.2
  488.3 36.3 %all-to-all-start = ((f32[32,4,1,128]{3,2,1,0:T(1,128)}), f32[32,4,1,128]{3,2,1,0:T(1,128)S(1)}, u32[]{:S(2)}, u32[]{:S(2)}) async-start(f32[32,4,1,128]{3,2,1,0:T(1,128)} %broadcast_in_dim.1314), calls=%async_computation | async-start | bytes 131072 | tf_op jit(solution)/shard_map/while/body/eval_jaxpr/all_to_all | solution.py:35
  501.5 6.1 %collective-permute-start = (f32[3,16,1]{2,1,0:T(8,128)S(1)}, f32[3,16,1]{2,1,0:T(8,128)S(1)}, u32[]{:S(2)}, u32[]{:S(2)}) collective-permute-start(f32[3,16,1]{2,1,0:T(8,128)S(1)} %get-tuple-element.341), channel_id=1, source_target_pairs={{8,0},{16,8},{24,16},{32,24},{40,32},{48,40},{56,48},{64,56},{72,6... | collective-permute-start | bytes 584 | tf_op jit(solution)/shard_map/while/body/eval_jaxpr/ppermute | solution.py:58
  505.6 6.2 %collective-permute-start.1 = (f32[3,16,1]{2,1,0:T(8,128)S(1)}, f32[3,16,1]{2,1,0:T(8,128)S(1)}, u32[]{:S(2)}, u32[]{:S(2)}) collective-permute-start(f32[3,16,1]{2,1,0:T(8,128)S(1)} %get-tuple-element.342), channel_id=1, source_target_pairs={{0,8},{8,16},{16,24},{24,32},{32,40},{40,48},{48,56},{56,64},{64,7... | collective-permute-start | bytes 584 | tf_op jit(solution)/shard_map/while/body/eval_jaxpr/ppermute | solution.py:56
  511.9 2.7 collective-permute-start.3
  513.9 4.5 collective-permute-start.2
  527.9 36.3 %all-to-all-start = ((f32[32,4,1,128]{3,2,1,0:T(1,128)}), f32[32,4,1,128]{3,2,1,0:T(1,128)S(1)}, u32[]{:S(2)}, u32[]{:S(2)}) async-start(f32[32,4,1,128]{3,2,1,0:T(1,128)} %broadcast_in_dim.1314), calls=%async_computation | async-start | bytes 131072 | tf_op jit(solution)/shard_map/while/body/eval_jaxpr/all_to_all | solution.py:35
  541.0 6.1 %collective-permute-start = (f32[3,16,1]{2,1,0:T(8,128)S(1)}, f32[3,16,1]{2,1,0:T(8,128)S(1)}, u32[]{:S(2)}, u32[]{:S(2)}) collective-permute-start(f32[3,16,1]{2,1,0:T(8,128)S(1)} %get-tuple-element.341), channel_id=1, source_target_pairs={{8,0},{16,8},{24,16},{32,24},{40,32},{48,40},{56,48},{64,56},{72,6... | collective-permute-start | bytes 584 | tf_op jit(solution)/shard_map/while/body/eval_jaxpr/ppermute | solution.py:58
  545.2 6.2 %collective-permute-start.1 = (f32[3,16,1]{2,1,0:T(8,128)S(1)}, f32[3,16,1]{2,1,0:T(8,128)S(1)}, u32[]{:S(2)}, u32[]{:S(2)}) collective-permute-start(f32[3,16,1]{2,1,0:T(8,128)S(1)} %get-tuple-element.342), channel_id=1, source_target_pairs={{0,8},{8,16},{16,24},{24,32},{32,40},{40,48},{48,56},{56,64},{64,7... | collective-permute-start | bytes 584 | tf_op jit(solution)/shard_map/while/body/eval_jaxpr/ppermute | solution.py:56
  553.4 4.5 collective-permute-start.2
  (15 other events, 187.5 us)
Sparse Core Ops, SparseCore 0:
  10.0 144.4 all-gather.1
where the time goes:
time: 595 us; the launch traced here: 591 us
  starting transfers between devices  305 us (51%)
  waiting for transfers between devices  198 us (33%)
  local copies, waits for them, and re-layouts  48.3 us (8%)
  other arithmetic  22.7 us (4%)
  between operations  15.1 us (3%)
    all_to_all x13, starting transfers between devices, from_everyone(): return lax.all_to_all(copies, axis, split_axis=0, concat_axis=0, tiled=True)  151 us
    all_to_all x13, waiting for transfers between devices, from_everyone(): return lax.all_to_all(copies, axis, split_axis=0, concat_axis=0, tiled=True)  93.3 us
    ppermute x24, waiting for transfers between devices, with_halo(): lax.ppermute(tail, axis, [(i, (i + 1) % count) for i in range(count)])  59.6 us
    ppermute x24, starting transfers between devices, with_halo(): lax.ppermute(head, axis, [((i + 1) % count, i) for i in range(count)])  50 us
    ppermute x24, starting transfers between devices, with_halo(): lax.ppermute(tail, axis, [(i, (i + 1) % count) for i in range(count)])  47.5 us
    ppermute x4, starting transfers between devices, padded(): lax.ppermute(last, axis, up)  47.2 us
    ppermute x24, waiting for transfers between devices, with_halo(): lax.ppermute(head, axis, [((i + 1) % count, i) for i in range(count)])  45.4 us
    gather x12, local copies, waits for them, and re-layouts, joint_cycle(): fold_vals = jnp.take(row_next, fold_pair)[None]  13.8 us
  transfers between devices with their start and end apart: 70, of which 49 were waited for; matrix products, arithmetic and copies ran while one was open for 11% of the time, Pallas kernels for 0%

commit v1 on v0

v1 whole, which is shorter than its diff:
```python
import functools

import jax
import jax.numpy as jnp
from jax import lax
from jax.experimental import pallas as pl
from jax.experimental.pallas import tpu as pltpu
from jax.sharding import PartitionSpec as P

SUB = 12
fb_step = 0.6
drag_rate = 0.02
MESH = pl.DeviceIdType.MESH

E, W, N, S, NE, NW, SE, SW = range(8)
OPPOSITE = {E: W, W: E, N: S, S: N, NE: SW, SW: NE, NW: SE, SE: NW}
STEP = {E: (0, 1), W: (0, -1), N: (1, 0), S: (-1, 0), NE: (1, 1), NW: (1, -1), SE: (-1, 1), SW: (-1, -1)}
REACH = (-3, -2, -1, 0, 1, 2, 3)
HOPS = (2, 4, 8)


def ocean_kernel(
    n_lon,
    n_lat,
    depth,
    rows,
    cols,
    tracer_hbm,
    velocity_hbm,
    surface_hbm,
    transport_hbm,
    levels_hbm,
    horiz,
    vert,
    land,
    fold,
    tracer_out,
    surface_out,
    transport_out,
    tr,
    vel,
    lev,
    own,
    halo,
    edge_lon,
    halo_lon,
    edge_lat,
    halo_lat,
    slab,
    hop_in,
    fin,
    tfin,
    step_ref,
    cpl,
    rec,
    prime,
    face_lat,
    mix_rows,
    ext,
    coef,
    fold_fix,
    load_sem,
    halo_send,
    halo_recv,
    trac_send,
    trac_recv,
    hop_send,
    hop_recv,
    fin_send,
    fin_recv,
    tfin_recv,
):
    lat = lax.axis_index("lat")
    lon = lax.axis_index("lon")
    top = lat == n_lat - 1
    bottom = lat == 0
    t_relay = n_lat - 3
    v_relay = 1
    is_t_relay = lat == t_relay
    is_v_relay = lat == v_relay
    relay = is_t_relay | is_v_relay

    def lon_at(step):
        return lax.rem(lon + step + n_lon, n_lon)

    def lat_at(step):
        return lax.rem(lat + step + n_lat, n_lat)

    def remote(src, dst, send, recv, to):
        return pltpu.make_async_remote_copy(
            src_ref=src, dst_ref=dst, send_sem=send, recv_sem=recv, device_id=to, device_id_type=MESH
        )

    small = [
        pltpu.make_async_copy(surface_hbm, own.at[pl.ds(0, rows)], load_sem.at[0]),
        pltpu.make_async_copy(transport_hbm, own.at[pl.ds(rows, 2 * rows)], load_sem.at[1]),
        pltpu.make_async_copy(levels_hbm, lev, load_sem.at[2]),
    ]
    large = [
        pltpu.make_async_copy(tracer_hbm, tr, load_sem.at[3]),
        pltpu.make_async_copy(velocity_hbm, vel, load_sem.at[4]),
    ]
    for copy in small:
        copy.start()
    barrier = pltpu.get_barrier_semaphore()
    peers = [STEP[side] for side in range(8)] + [(0, 2), (0, -2), (2, 0), (-2, 0)]
    for d_lat, d_lon in peers:
        pl.semaphore_signal(
            barrier, inc=1, device_id={"lat": lat_at(d_lat), "lon": lon_at(d_lon)}, device_id_type=MESH
        )
    for copy in large:
        copy.start()

    zeros_tile = jnp.zeros((4 * rows, cols), jnp.float32)

    @pl.when(bottom)
    def _():
        for side in (S, SE, SW):
            halo[side] = zeros_tile
        halo_lat[1] = jnp.zeros((2 * depth, cols), jnp.float32)

    @pl.when(top)
    def _():
        halo[N] = zeros_tile
        halo_lat[0] = jnp.zeros((2 * depth, cols), jnp.float32)

    for copy in small:
        copy.wait()
    dry = 1 - land[0, 0]
    own[pl.ds(3 * rows, rows), :] = (lev[...] * dry).astype(jnp.float32)

    @pl.when(top)
    def _():
        slab[0] = zeros_tile
        for i in range(12):
            last = rows - 1 - i
            slab[0, pl.ds(i, 1), :] = own[pl.ds(last, 1), :]
            slab[0, pl.ds(rows + i, 1), :] = -own[pl.ds(rows + last, 1), :]
            slab[0, pl.ds(2 * rows + i, 1), :] = own[pl.ds(3 * rows + last, 1), :]
            slab[0, pl.ds(3 * rows + i, 1), :] = -own[pl.ds(2 * rows + last - 1, 1), :]
        slab[0, pl.ds(3 * rows + 12, 1), :] = -own[pl.ds(3 * rows - 1, 1), :]

    pl.semaphore_wait(barrier, len(peers))

    def hop_copies(k, size):
        out = []
        for j, sign in enumerate((1, -1)):
            out.append(
                remote(
                    slab.at[k, pl.ds(0, size)],
                    hop_in.at[2 * k + j, pl.ds(0, size)],
                    hop_send.at[2 * k + j],
                    hop_recv.at[2 * k + j],
                    {"lon": lon_at(sign * HOPS[k])},
                )
            )
        return out

    pivot_col = lax.rem(fold[0] + lon * cols, n_lon * cols)
    q = pivot_col // cols
    r = pivot_col - q * cols
    q_odd = q - 1 + (q & 1)

    def turn(m):
        return ((q_odd - 2 * m + 15 + 4 * n_lon) & (n_lon - 1)) >> 1

    tau = turn(lon)

    def hop_start(k, size):
        for copy in hop_copies(k, size):
            copy.start()

    def hop_next(k, size):
        for copy in hop_copies(k, size):
            copy.wait_recv()
        bit = jnp.full((size, cols), (tau >> (k + 1)) & 1, jnp.int32)
        slab[k + 1, pl.ds(0, size), :] = jnp.where(
            bit == 0, hop_in[2 * k, pl.ds(0, size), :], hop_in[2 * k + 1, pl.ds(0, size), :]
        )

    @pl.when(top)
    def _():
        hop_start(0, 4 * rows)

    def halo_copy(side):
        d_lat, d_lon = STEP[side]
        slot = OPPOSITE[side]
        return remote(
            own,
            halo.at[slot],
            halo_send.at[side],
            halo_recv.at[slot],
            {"lat": lat_at(d_lat), "lon": lon_at(d_lon)},
        )

    def halo_wait(side):
        remote(own, halo.at[side], halo_send.at[side], halo_recv.at[side], {"lon": lon}).wait_recv()

    for side in (E, W):
        halo_copy(side).start()

    @pl.when(jnp.logical_not(top))
    def _():
        for side in (N, NE, NW):
            halo_copy(side).start()

    @pl.when(jnp.logical_not(bottom))
    def _():
        for side in (S, SE, SW):
            halo_copy(side).start()

    for copy in large:
        copy.wait()
    u_base = 0
    v_base = depth * rows
    edge_lat[0, pl.ds(0, depth), :] = tr[pl.ds(rows - 1, depth, stride=rows), :]
    edge_lat[0, pl.ds(depth, depth), :] = vel[pl.ds(v_base + rows - 1, depth, stride=rows), :]
    edge_lat[1, pl.ds(0, depth), :] = tr[pl.ds(0, depth, stride=rows), :]
    edge_lat[1, pl.ds(depth, depth), :] = vel[pl.ds(v_base, depth, stride=rows), :]

    def spread_copy(j):
        to = (t_relay, v_relay)[j]
        return remote(
            edge_lat.at[0, pl.ds(j * depth, depth)],
            slab.at[0, pl.ds(0, depth)],
            trac_send.at[j],
            trac_recv.at[4],
            {"lat": to},
        )

    def lat_copy(north):
        slot = 1 if north else 0
        return remote(
            edge_lat.at[0 if north else 1],
            halo_lat.at[slot],
            trac_send.at[0 if north else 2],
            trac_recv.at[slot],
            {"lat": lat_at(1 if north else -1)},
        )

    @pl.when(top)
    def _():
        spread_copy(0).start()
        spread_copy(1).start()

    @pl.when(jnp.logical_not(top))
    def _():
        lat_copy(True).start()

    @pl.when(jnp.logical_not(bottom))
    def _():
        lat_copy(False).start()

    lane8 = lax.broadcasted_iota(jnp.int32, (8, cols), 1)
    half = lane8 >> 1

    def pack(l, carry):
        pt, pu = carry
        for g in range(2):
            item = l + depth * g
            here = half == jnp.full((8, cols), item, jnp.int32)
            at = pl.multiple_of(l * rows + 8 * g, 8)
            pt = jnp.where(here, pltpu.roll(tr[pl.ds(at, 8), :], 2 * item + 1, axis=1), pt)
            pu = jnp.where(here, pltpu.roll(vel[pl.ds(at, 8), :], 2 * item + 1, axis=1), pu)
        return pt, pu

    pt, pu = lax.fori_loop(
        0, depth, pack, (jnp.zeros((8, cols), jnp.float32), jnp.zeros((8, cols), jnp.float32)), unroll=4
    )
    edge_lon[pl.ds(0, 8), :] = pt
    edge_lon[pl.ds(8, 8), :] = pu

    def lon_copy(east):
        slot = 1 if east else 0
        return remote(
            edge_lon,
            halo_lon.at[slot],
            trac_send.at[3 if east else 4],
            trac_recv.at[2 + slot],
            {"lon": lon_at(1 if east else -1)},
        )

    lon_copy(True).start()
    lon_copy(False).start()

    def trac_wait(dst, sem):
        remote(dst, dst, trac_send.at[5], sem, {"lon": lon}).wait_recv()

    @pl.when(relay)
    def _():
        trac_wait(slab.at[0, pl.ds(0, depth)], trac_recv.at[4])
        hop_start(0, depth)

    h_own = own[pl.ds(3 * rows, rows), :]

    def pivots(l, carry):
        c_up, p_up = carry
        wet_below = (jnp.full((rows, cols), (l + 1).astype(jnp.float32)) < h_own).astype(jnp.float32)
        c_down = vert[jnp.minimum(l, depth - 2)] * wet_below
        pivot = (1.0 + c_up + c_down) + c_up * p_up
        inv = 1.0 / pivot
        p_down = -c_down * inv
        at = pl.ds(pl.multiple_of(l * rows, rows), rows)
        cpl[at, :] = c_up
        rec[at, :] = inv
        prime[at, :] = p_down
        mix_rows[pl.ds(l, 1), :] = jnp.full((1, cols), horiz[l])
        return c_down, p_down

    zero = jnp.zeros((rows, cols), jnp.float32)
    lax.fori_loop(0, depth, pivots, (zero, zero), unroll=2)

    @pl.when(top)
    def _():
        hop_next(0, 4 * rows)
        hop_start(1, 4 * rows)

    @pl.when(relay)
    def _():
        hop_next(0, depth)
        hop_start(1, depth)

    for side in (E, W):
        halo_wait(side)

    @pl.when(jnp.logical_not(top))
    def _():
        for side in (N, NE, NW):
            halo_wait(side)

    @pl.when(jnp.logical_not(bottom))
    def _():
        for side in (S, SE, SW):
            halo_wait(side)

    lane16 = lax.broadcasted_iota(jnp.int32, (rows, cols), 1)
    row16 = lax.broadcasted_iota(jnp.int32, (rows, cols), 0)
    near = lane16 < cols // 2
    left, right = pl.ds(0, cols), pl.ds(cols, cols)
    for f in range(4):
        part = pl.ds(f * rows, rows)
        ext[f, pl.ds(0, rows), left] = halo[S, part, :]
        ext[f, pl.ds(0, rows), right] = jnp.where(near, halo[SE, part, :], halo[SW, part, :])
        ext[f, pl.ds(rows, rows), left] = own[part, :]
        ext[f, pl.ds(rows, rows), right] = jnp.where(near, halo[E, part, :], halo[W, part, :])

    fold_fix[...] = jnp.zeros((8, 2 * cols), jnp.float32)

    @pl.when(jnp.logical_not(top))
    def _():
        for f in range(4):
            part = pl.ds(f * rows, rows)
            ext[f, pl.ds(2 * rows, rows), left] = halo[N, part, :]
            ext[f, pl.ds(2 * rows, rows), right] = jnp.where(near, halo[NE, part, :], halo[NW, part, :])

    @pl.when(top)
    def _():
        hop_next(1, 4 * rows)
        hop_start(2, 4 * rows)

    @pl.when(relay)
    def _():
        hop_next(1, depth)
        hop_start(2, depth)

    trac_wait(halo_lon.at[0], trac_recv.at[2])
    trac_wait(halo_lon.at[1], trac_recv.at[3])

    @pl.when(jnp.logical_not(top))
    def _():
        trac_wait(halo_lat.at[0], trac_recv.at[0])

    @pl.when(jnp.logical_not(bottom))
    def _():
        trac_wait(halo_lat.at[1], trac_recv.at[1])

    even = (lane8 & 1) == 0
    h_east_tile = halo[E, pl.ds(3 * rows, rows), :]
    h_west_tile = halo[W, pl.ds(3 * rows, rows), :]
    h_north_row = halo[N, pl.ds(3 * rows, 1), :]
    h_south_row = halo[S, pl.ds(4 * rows - 1, 1), :]

    def swap(from_east, from_west):
        return jnp.where(
            even, pltpu.roll(from_east, cols - 1, axis=1), pltpu.roll(from_west, 1, axis=1)
        )

    pt = edge_lon[pl.ds(0, 8), :]
    pu = edge_lon[pl.ds(8, 8), :]
    th = swap(halo_lon[0, pl.ds(0, 8), :], halo_lon[1, pl.ds(0, 8), :])
    uh = swap(halo_lon[0, pl.ds(8, 8), :], halo_lon[1, pl.ds(8, 8), :])

    def column(tile, at):
        lo = jnp.broadcast_to(tile[0:8, at : at + 1], (8, cols))
        hi = jnp.broadcast_to(tile[8:16, at : at + 1], (8, cols))
        return jnp.where(half < depth, lo, hi)

    level_of = (half & (depth - 1)).astype(jnp.float32)
    h_in = jnp.where(even, column(h_own, cols - 1), column(h_own, 0))
    h_out = jnp.where(even, column(h_east_tile, 0), column(h_west_tile, cols - 1))
    wet_pair = (level_of < h_in).astype(jnp.float32) * (level_of < h_out).astype(jnp.float32)

    def lane_mix(l, acc):
        return jnp.where((half & (depth - 1)) == jnp.full((8, cols), l, jnp.int32), horiz[l], acc)

    mix_lanes = lax.fori_loop(0, depth, lane_mix, jnp.zeros((8, cols), jnp.float32), unroll=4)
    signed = jnp.where(even, th - pt, pt - th)
    side_flux = wet_pair * (mix_lanes * signed - 0.25 * (pu + uh) * (pt + th))

    level_row = lax.broadcasted_iota(jnp.int32, (depth, cols), 0).astype(jnp.float32)

    def row_face(low_t, low_v, high_t, high_v, h_low, h_high):
        wet = (level_row < h_low).astype(jnp.float32) * (level_row < h_high).astype(jnp.float32)
        return wet * (mix_rows[...] * (high_t - low_t) - 0.25 * (low_v + high_v) * (low_t + high_t))

    first, second = pl.ds(0, depth), pl.ds(depth, depth)
    face_lat[0] = row_face(
        edge_lat[0, first, :], edge_lat[0, second, :], halo_lat[0, first, :], halo_lat[0, second, :],
        own[pl.ds(4 * rows - 1, 1), :], h_north_row,
    )
    face_lat[1] = row_face(
        halo_lat[1, first, :], halo_lat[1, second, :], edge_lat[1, first, :], edge_lat[1, second, :],
        h_south_row, own[pl.ds(3 * rows, 1), :],
    )

    last_col = lane16 == cols - 1
    first_col = lane16 == 0
    last_row = row16 == rows - 1
    first_row = row16 == 0
    h_e = pltpu.roll(h_own, cols - 1, axis=1)
    h_n = pltpu.roll(h_own, rows - 1, axis=0)

    def fluxes(l, carry):
        at = pl.ds(pl.multiple_of(l * rows, rows), rows)
        t = tr[at, :]
        u = vel[at, :]
        v = vel[pl.ds(pl.multiple_of(v_base + l * rows, rows), rows), :]
        m = horiz[l]
        level = jnp.full((rows, cols), l.astype(jnp.float32))
        wet = (level < h_own).astype(jnp.float32)
        wet_e = (level < h_e).astype(jnp.float32)
        wet_n = (level < h_n).astype(jnp.float32)
        t_e = pltpu.roll(t, cols - 1, axis=1)
        u_e = pltpu.roll(u, cols - 1, axis=1)
        f_e = wet * wet_e * (m * (t_e - t) - 0.25 * (u + u_e) * (t + t_e))
        rim = jnp.concatenate(
            [
                pltpu.roll(side_flux, cols - 1 - 2 * l, axis=1),
                pltpu.roll(side_flux, lax.rem(2 * cols - 1 - 2 * (l + depth), cols), axis=1),
            ],
            axis=0,
        )
        f_e = jnp.where(last_col, rim, f_e)
        f_w = jnp.where(first_col, rim, pltpu.roll(f_e, 1, axis=1))
        t_n = pltpu.roll(t, rows - 1, axis=0)
        v_n = pltpu.roll(v, rows - 1, axis=0)
        f_n = wet * wet_n * (m * (t_n - t) - 0.25 * (v + v_n) * (t + t_n))
        f_n = jnp.where(last_row, face_lat[0, pl.ds(l, 1), :], f_n)
        f_s = jnp.where(first_row, face_lat[1, pl.ds(l, 1), :], pltpu.roll(f_n, 1, axis=0))
        step_ref[at, :] = wet * (t + ((f_e - f_w) + (f_n - f_s)))
        return carry

    lax.fori_loop(0, depth, fluxes, 0, unroll=4)

    def forward(l, sweep):
        at = pl.ds(pl.multiple_of(l * rows, rows), rows)
        sweep = (step_ref[at, :] + cpl[at, :] * sweep) * rec[at, :]
        step_ref[at, :] = sweep
        return sweep

    lax.fori_loop(0, depth, forward, zero, unroll=4)

    def backward(i, x):
        l = depth - 1 - i
        at = pl.ds(pl.multiple_of(l * rows, rows), rows)
        x = step_ref[at, :] - prime[at, :] * x
        tracer_out[at, :] = x
        return x

    lax.fori_loop(0, depth, backward, zero, unroll=4)

    def final_copy(i, size, dst, recv):
        return remote(
            slab.at[3, pl.ds(0, size)],
            dst,
            fin_send.at[i],
            recv,
            {"lat": n_lat - 1, "lon": lon_at(REACH[i])},
        )

    @pl.when(top)
    def _():
        hop_next(2, 4 * rows)
        for i, e in enumerate(REACH):
            if e:
                final_copy(i, 4 * rows, fin.at[i], fin_recv.at[i]).start()

    @pl.when(is_t_relay)
    def _():
        hop_next(2, depth)
        for i in range(len(REACH)):
            final_copy(i, depth, tfin.at[0, i], tfin_recv.at[0, i]).start()

    @pl.when(is_v_relay)
    def _():
        hop_next(2, depth)
        for i in range(len(REACH)):
            final_copy(i, depth, tfin.at[1, i], tfin_recv.at[1, i]).start()

    def source(e):
        m = lon_at(-e)
        sigma = q_odd - m + 1 - 2 * (turn(m) & 1)
        return (sigma + 2 * n_lon) & (n_lon - 1)

    sources = [source(e) for e in REACH]

    def source_of(shape, shift, isu):
        s = lax.broadcasted_iota(jnp.int32, shape, 1)
        l = (jnp.full(shape, r, jnp.int32) - isu - s) & (cols - 1)
        return s, l

    @pl.when(top)
    def _():
        for i, e in enumerate(REACH):
            if e:
                final_copy(i, 4 * rows, fin.at[i], fin_recv.at[i]).wait_recv()
        shape = (4 * rows, cols)
        row = lax.broadcasted_iota(jnp.int32, shape, 0)
        isu = ((row >= rows) & (row < 2 * rows)).astype(jnp.int32)
        s, l = source_of(shape, 0, isu)
        whole = n_lon * cols
        base = jnp.full(shape, pivot_col - lon * cols + 2 * whole, jnp.int32) - isu
        dev_main = ((base - l) & (whole - 1)) >> 7
        off = jnp.where(l < cols // 2, cols, -cols)
        dev_side = ((base - l - off) & (whole - 1)) >> 7
        main = zeros_tile
        side = zeros_tile
        for i, e in enumerate(REACH):
            got = fin[i] if e else slab[3]
            src = jnp.full(shape, sources[i], jnp.int32)
            main = jnp.where(dev_main == src, got, main)
            side = jnp.where(dev_side == src, got, side)
        main = jnp.take_along_axis(main, l, axis=1)
        side = jnp.take_along_axis(side, l, axis=1)
        for f in range(4):
            ff = (0, 1, 3, 2)[f]
            ext[ff, pl.ds(2 * rows, rows), left] = main[f * rows : (f + 1) * rows]
            ext[ff, pl.ds(2 * rows, rows), right] = side[f * rows : (f + 1) * rows]
        fold_fix[pl.ds(0, 1), left] = main[3 * rows + 12 : 3 * rows + 13] - ext[2, pl.ds(2 * rows - 1, 1), left]
        fold_fix[pl.ds(0, 1), right] = side[3 * rows + 12 : 3 * rows + 13] - ext[2, pl.ds(2 * rows - 1, 1), right]

    wide = 2 * cols
    tall = 3 * rows
    h = ext[3]
    sea = (h > 0.0).astype(jnp.float32)

    def east(x):
        return pltpu.roll(x, wide - 1, axis=1)

    def north(x):
        return pltpu.roll(x, tall - 1, axis=0)

    zonal_mask = sea * east(sea)
    merid_mask = sea * north(sea)
    coef[0] = fb_step * ((h + east(h)) / (2.0 * depth)) * zonal_mask
    coef[1] = (1.0 - drag_rate) * zonal_mask
    coef[2] = fb_step * ((h + north(h)) / (2.0 * depth)) * merid_mask
    coef[3] = (1.0 - drag_rate) * merid_mask
    coef[4] = fb_step * sea
    fix_decay = pltpu.roll(coef[3], 1, axis=0)[2 * rows : 2 * rows + 8]

    def cycle(i, state):
        eta, u, v, fix = state
        v_south = pltpu.roll(v, 1, axis=0)
        v_south = jnp.concatenate(
            [v_south[: 2 * rows], v_south[2 * rows : 2 * rows + 8] + fix, v_south[2 * rows + 8 :]], axis=0
        )
        div = (u - pltpu.roll(u, 1, axis=1)) + (v - v_south)
        eta = eta - coef[4] * div
        u = u * coef[1] - coef[0] * (east(eta) - eta)
        v = v * coef[3] - coef[2] * (north(eta) - eta)
        return eta, u, v, fix * fix_decay

    eta, u, v, _ = lax.fori_loop(0, SUB, cycle, (ext[0] * sea, ext[1], ext[2], fold_fix[...]))
    surface_out[...] = eta[rows : 2 * rows, :cols]
    transport_out[pl.ds(0, rows), :] = u[rows : 2 * rows, :cols]
    transport_out[pl.ds(rows, rows), :] = v[rows : 2 * rows, :cols]

    @pl.when(top)
    def _():
        got = []
        for j in range(2):
            shape = (depth, cols)
            s, l = source_of(shape, 0, 0)
            whole = n_lon * cols
            dev = ((jnp.full(shape, pivot_col - lon * cols + 2 * whole, jnp.int32) - l) & (whole - 1)) >> 7
            acc = jnp.zeros(shape, jnp.float32)
            for i in range(len(REACH)):
                trac_wait(tfin.at[j, i], tfin_recv.at[j, i])
                acc = jnp.where(dev == jnp.full(shape, sources[i], jnp.int32), tfin[j, i], acc)
            got.append(jnp.take_along_axis(acc, l, axis=1))
        h_last = own[pl.ds(4 * rows - 1, 1), :]
        flux = row_face(
            edge_lat[0, first, :], edge_lat[0, second, :], got[0], got[1], h_last, ext[3, pl.ds(2 * rows, 1), left]
        )
        face_lat[0] = (level_row < h_last).astype(jnp.float32) * flux
        c_last = cpl[pl.ds(rows - 1, depth, stride=rows), :]
        r_last = rec[pl.ds(rows - 1, depth, stride=rows), :]
        p_last = prime[pl.ds(rows - 1, depth, stride=rows), :]
        out_last = tracer_out[pl.ds(rows - 1, depth, stride=rows), :]
        delta = face_lat[0]
        sweeps = []
        x = jnp.zeros((1, cols), jnp.float32)
        for k in range(depth):
            x = (delta[k : k + 1] + c_last[k : k + 1] * x) * r_last[k : k + 1]
            sweeps.append(x)
        x = jnp.zeros((1, cols), jnp.float32)
        for k in range(depth - 1, -1, -1):
            x = sweeps[k] - p_last[k : k + 1] * x
            tracer_out[pl.ds(k * rows + rows - 1, 1), :] = out_last[k : k + 1] + x

    for side in (E, W):
        halo_copy(side).wait_send()
    lon_copy(True).wait_send()
    lon_copy(False).wait_send()

    @pl.when(jnp.logical_not(top))
    def _():
        for side in (N, NE, NW):
            halo_copy(side).wait_send()
        lat_copy(True).wait_send()

    @pl.when(jnp.logical_not(bottom))
    def _():
        for side in (S, SE, SW):
            halo_copy(side).wait_send()
        lat_copy(False).wait_send()

    @pl.when(top)
    def _():
        spread_copy(0).wait_send()
        spread_copy(1).wait_send()
        for k in range(3):
            for copy in hop_copies(k, 4 * rows):
                copy.wait_send()
        for i, e in enumerate(REACH):
            if e:
                final_copy(i, 4 * rows, fin.at[i], fin_recv.at[i]).wait_send()

    @pl.when(relay)
    def _():
        for k in range(3):
            for copy in hop_copies(k, depth):
                copy.wait_send()
        for i in range(len(REACH)):
            final_copy(i, depth, tfin.at[0, i], tfin_recv.at[0, i]).wait_send()


def solution(mesh):
    n_lon, n_lat = mesh.shape["lon"], mesh.shape["lat"]

    def shards(tracer, velocity, surface, transport, horiz_mixing, vert_mixing, levels, land_tiles, fold_pair):
        depth, rows, cols = tracer.shape
        f32 = jnp.float32
        hbm = pl.BlockSpec(memory_space=pl.ANY)
        smem = pl.BlockSpec(memory_space=pltpu.SMEM)
        vmem = pl.BlockSpec(memory_space=pltpu.VMEM)
        dma = pltpu.SemaphoreType.DMA
        field = pltpu.VMEM((depth * rows, cols), f32)
        tracer_new, surface_new, transport_new = pl.pallas_call(
            functools.partial(ocean_kernel, n_lon, n_lat, depth, rows, cols),
            name="ocean",
            out_shape=(
                jax.ShapeDtypeStruct((depth * rows, cols), f32),
                jax.ShapeDtypeStruct((rows, cols), f32),
                jax.ShapeDtypeStruct((2 * rows, cols), f32),
            ),
            in_specs=[hbm] * 5 + [smem] * 4,
            out_specs=(vmem, vmem, vmem),
            scratch_shapes=[
                field,
                pltpu.VMEM((2 * depth * rows, cols), f32),
                pltpu.VMEM((rows, cols), jnp.int32),
                pltpu.VMEM((4 * rows, cols), f32),
                pltpu.VMEM((8, 4 * rows, cols), f32),
                pltpu.VMEM((16, cols), f32),
                pltpu.VMEM((2, 16, cols), f32),
                pltpu.VMEM((2, 2 * depth, cols), f32),
                pltpu.VMEM((2, 2 * depth, cols), f32),
                pltpu.VMEM((4, 4 * rows, cols), f32),
                pltpu.VMEM((6, 4 * rows, cols), f32),
                pltpu.VMEM((7, 4 * rows, cols), f32),
                pltpu.VMEM((2, 7, depth, cols), f32),
                field,
                field,
                field,
                field,
                pltpu.VMEM((2, depth, cols), f32),
                pltpu.VMEM((depth, cols), f32),
                pltpu.VMEM((4, 3 * rows, 2 * cols), f32),
                pltpu.VMEM((5, 3 * rows, 2 * cols), f32),
                pltpu.VMEM((8, 2 * cols), f32),
                dma((5,)),
                dma((8,)),
                dma((8,)),
                dma((6,)),
                dma((5,)),
                dma((6,)),
                dma((6,)),
                dma((7,)),
                dma((7,)),
                dma((2, 7)),
            ],
            compiler_params=pltpu.CompilerParams(collective_id=1, has_side_effects=True),
        )(
            tracer.reshape(depth * rows, cols),
            velocity.reshape(2 * depth * rows, cols),
            surface,
            transport.reshape(2 * rows, cols),
            levels,
            horiz_mixing,
            vert_mixing,
            land_tiles,
            fold_pair,
        )
        return (
            tracer_new.reshape(depth, rows, cols),
            surface_new,
            transport_new.reshape(2, rows, cols),
        )

    return jax.shard_map(
        shards,
        mesh=mesh,
        in_specs=(
            P("member", "lat", "lon"),
            P(None, "member", "lat", "lon"),
            P(("member", "lat"), "lon"),
            P("member", "lat", "lon"),
            P("member"),
            P("member"),
            P("lat", "lon"),
            P("lat", "lon"),
            P("lon"),
        ),
        out_specs=(
            P("member", "lat", "lon"),
            P(("member", "lat"), "lon"),
            P("member", "lat", "lon"),
        ),
        check_vma=False,
    )
```

time: 595 us -> 72.6 us (0.12)
  starting transfers between devices: 305 us -> 0 us
  waiting for transfers between devices: 198 us -> 0 us
  Pallas kernels: 0 us -> 68 us
  local copies, waits for them, and re-layouts: 48.3 us -> 3.01 us
  other arithmetic: 22.7 us -> 0 us
  between operations: 15.1 us -> 1.3 us
    ppermute x56 -> x0, starting transfers between devices: 154 us -> none  [the longest x24 50 us: with_halo(): lax.ppermute(head, axis, [((i + 1) % count, i) for i in range(count)])]
    all_to_all x13 -> x0, starting transfers between devices: 151 us -> none  [from_everyone(): return lax.all_to_all(copies, axis, split_axis=0, concat_axis=0, tiled=True)]
    ppermute x56 -> x0, waiting for transfers between devices: 105 us -> none  [the longest x24 59.6 us: with_halo(): lax.ppermute(tail, axis, [(i, (i + 1) % count) for i in range(count)])]
    all_to_all x13 -> x0, waiting for transfers between devices: 93.3 us -> none  [from_everyone(): return lax.all_to_all(copies, axis, split_axis=0, concat_axis=0, tiled=True)]
    pallas_call x0 -> x1, Pallas kernels: none -> 68 us  [shards(): pl.pallas_call(functools.partial(ocean_kernel, n_lon, n_lat, depth, rows,...]
    gather x14 -> x0, local copies, waits for them, and re-layouts: 19.1 us -> none  [the longest x12 13.8 us: joint_cycle(): fold_vals = jnp.take(row_next, fold_pair)[None]]
    mul x54 -> x0, other arithmetic: 13.7 us -> none  [the longest x12 8.68 us: joint_cycle(): row_next = (row_height - fb_step * row_div) * sea_top_row]
    broadcast_in_dim x13 -> x0, local copies, waits for them, and re-layouts: 8.59 us -> none  [from_everyone(): copies = jnp.broadcast_to(shard, (lax.axis_size(axis), *shard.shape))]
  transfers between devices with their start and end apart: 70 -> 0, of which waited for: 49 -> 0; matrix products, arithmetic and copies ran while one was open for 11% -> 0% of each run, Pallas kernels for 0% -> 0%
where the time goes in v1:
time: 72.6 us; the launch traced here: 72.3 us
  Pallas kernels  68 us (94%)
  local copies, waits for them, and re-layouts  3.01 us (4%)
  between operations  1.3 us (2%)
    pallas_call x1, Pallas kernels, shards(): pl.pallas_call(functools.partial(ocean_kernel, n_lon, n_lat, depth, rows,...  68 us
    unnamed x7, local copies, waits for them, and re-layouts  3.01 us

profile of v1, /device:TPU:39, one launch (start us, length us, event | category | flops | bytes accessed | tf_op | source)
XLA Modules:
  0.0 72.3 jit_solution(9986190485554939821)
XLA Ops:
  1.3 68.0 %ocean.1 = (f32[512,128]{1,0:T(8,128)}, f32[16,128]{1,0:T(8,128)}, f32[32,128]{1,0:T(8,128)}) custom-call(f32[512,128]{1,0:T(8,128)} %bitcast.6, f32[1024,128]{1,0:T(8,128)} %bitcast.5, f32[16,128]{1,0:T(8,128)} %surface_hbm.1, f32[32,128]{1,0:T(8,128)} %bitcast.8, s32[16,128]{1,0:T(8,128)} %levels_hbm.1, f32[32]{0:T(128)} %horiz.1, f32[31]{0:T(128)} %vert.1, ...), custom_call_target="tpu_custom_call" | custom-call | tf_op jit(solution)/shard_map/ocean/pallas_call | solution.py:670
  69.3 0.0 copy-start.1
  69.3 1.7 %copy.16 = f32[32,16,128]{2,1,0:T(8,128)} copy(f32[32,16,128]{2,1,0:T(8,128)} %bitcast.7) | data formatting | bytes 524288
  71.0 0.0 copy-done.1
  71.0 0.0 copy-start
  71.0 0.6 copy.17
  71.6 0.1 copy-done
  71.7 0.6 copy.18
Async XLA Ops:
  69.3 1.7 %copy-start.1 = (f32[16,128]{1,0:T(8,128)S(1)}, f32[16,128]{1,0:T(8,128)}, u32[]{:S(2)}) copy-start(f32[16,128]{1,0:T(8,128)} %get-tuple-element.13) | copy-start | bytes 24580
  71.0 0.7 copy-start

commit v2 on v1

v2 whole, which is shorter than its diff:
```python
import functools

import jax
import jax.numpy as jnp
from jax import lax
from jax.experimental import pallas as pl
from jax.experimental.pallas import tpu as pltpu
from jax.sharding import PartitionSpec as P

SUB = 12
fb_step = 0.6
drag_rate = 0.02
MESH = pl.DeviceIdType.MESH

E, W, N, S, NE, NW, SE, SW = range(8)
OPPOSITE = {E: W, W: E, N: S, S: N, NE: SW, SW: NE, NW: SE, SE: NW}
STEP = {E: (0, 1), W: (0, -1), N: (1, 0), S: (-1, 0), NE: (1, 1), NW: (1, -1), SE: (-1, 1), SW: (-1, -1)}
GROUP = 4


def ocean_kernel(
    n_lon,
    n_lat,
    depth,
    rows,
    cols,
    tracer_hbm,
    velocity_hbm,
    surface_hbm,
    transport_hbm,
    levels_hbm,
    horiz_hbm,
    vert_hbm,
    land_hbm,
    fold_hbm,
    tracer_out,
    surface_out,
    transport_out,
    horiz,
    vert,
    land,
    fold,
    tr,
    vel,
    lev,
    own,
    halo,
    side_out,
    side_in,
    edge_lon,
    halo_lon,
    edge_lat,
    halo_lat,
    slab,
    hold,
    fwd_out,
    fwd_in,
    pick,
    fin,
    tfin,
    step_ref,
    cpl,
    rec,
    prime,
    face_lat,
    mix_rows,
    ext,
    coef,
    fold_fix,
    load_sem,
    halo_send,
    halo_recv,
    trac_send,
    trac_recv,
    hold_send,
    hold_recv,
    fwd_send,
    fwd_recv,
    fin_send,
    fin_recv,
    tfin_recv,
):
    lat = lax.axis_index("lat")
    lon = lax.axis_index("lon")
    top = lat == n_lat - 1
    bottom = lat == 0
    t_relay = n_lat - 3
    v_relay = 1
    is_t_relay = lat == t_relay
    is_v_relay = lat == v_relay
    relay = is_t_relay | is_v_relay
    ring = top | relay
    n_group = n_lon // GROUP
    me = lon & (GROUP - 1)
    group = lon - me
    keeper = lon < GROUP
    half_way = n_group // 2
    at_group = lon >> 2
    rising = at_group <= half_way
    blocks = jnp.where(rising, half_way + 2 - at_group, half_way + 1 - n_group + at_group)
    onward = jnp.where(rising, GROUP, -GROUP)
    has_next = jnp.logical_not(keeper) & (blocks > 2)
    has_previous = (at_group > 1) & (at_group < n_group - 1)

    def partner(g):
        return g * GROUP + (GROUP - 1 - me)

    def lon_at(step):
        return lax.rem(lon + step + n_lon, n_lon)

    def lat_at(step):
        return lax.rem(lat + step + n_lat, n_lat)

    def remote(src, dst, send, recv, to):
        return pltpu.make_async_remote_copy(
            src_ref=src, dst_ref=dst, send_sem=send, recv_sem=recv, device_id=to, device_id_type=MESH
        )

    small = [
        pltpu.make_async_copy(surface_hbm, own.at[pl.ds(0, rows)], load_sem.at[0]),
        pltpu.make_async_copy(transport_hbm, own.at[pl.ds(rows, 2 * rows)], load_sem.at[1]),
        pltpu.make_async_copy(levels_hbm, lev, load_sem.at[2]),
        pltpu.make_async_copy(land_hbm, land, load_sem.at[5]),
        pltpu.make_async_copy(fold_hbm, fold, load_sem.at[6]),
        pltpu.make_async_copy(horiz_hbm, horiz, load_sem.at[7]),
        pltpu.make_async_copy(vert_hbm, vert, load_sem.at[8]),
    ]
    large = [
        pltpu.make_async_copy(tracer_hbm, tr, load_sem.at[3]),
        pltpu.make_async_copy(velocity_hbm, vel, load_sem.at[4]),
    ]
    for copy in small:
        copy.start()
    barrier = pltpu.get_barrier_semaphore()
    peers = [STEP[side] for side in range(8)] + [(2, 0), (-2, 0)]
    for d_lat, d_lon in peers:
        pl.semaphore_signal(
            barrier, inc=1, device_id={"lat": lat_at(d_lat), "lon": lon_at(d_lon)}, device_id_type=MESH
        )

    @pl.when(ring)
    def _():
        @pl.when(keeper)
        def _():
            for g in range(1, n_group):
                pl.semaphore_signal(barrier, inc=1, device_id={"lon": partner(g)}, device_id_type=MESH)

        @pl.when(has_previous)
        def _():
            pl.semaphore_signal(barrier, inc=1, device_id={"lon": lon - onward}, device_id_type=MESH)

        for e in range(1, GROUP):
            pl.semaphore_signal(
                barrier, inc=1, device_id={"lon": group + ((me + e) & (GROUP - 1))}, device_id_type=MESH
            )

    for copy in large:
        copy.start()

    zeros_tile = jnp.zeros((4 * rows, cols), jnp.float32)

    @pl.when(bottom)
    def _():
        halo[1] = zeros_tile
        for side in (SE, SW):
            side_in[side] = jnp.zeros((8, cols), jnp.float32)
        halo_lat[1] = jnp.zeros((2 * depth, cols), jnp.float32)

    @pl.when(top)
    def _():
        halo[0] = zeros_tile
        for side in (NE, NW):
            side_in[side] = jnp.zeros((8, cols), jnp.float32)
        halo_lat[0] = jnp.zeros((2 * depth, cols), jnp.float32)

    for copy in small:
        copy.wait()
    dry = 1 - land[0, 0]
    own[pl.ds(3 * rows, rows), :] = (lev[...] * dry).astype(jnp.float32)

    lane8 = lax.broadcasted_iota(jnp.int32, (8, cols), 1)
    to_east, to_west = jnp.zeros((8, cols), jnp.float32), jnp.zeros((8, cols), jnp.float32)
    for k in range(8):
        here = (lane8 >> 4) == k
        part = own[pl.ds(8 * k, 8), :]
        to_east = jnp.where(here, pltpu.roll(part, (16 * k + 16) % cols, axis=1), to_east)
        to_west = jnp.where(here, pltpu.roll(part, 16 * k, axis=1) if k else part, to_west)
    side_out[0] = to_east
    side_out[1] = to_west

    @pl.when(top)
    def _():
        slab[...] = zeros_tile
        for i in range(12):
            last = rows - 1 - i
            slab[pl.ds(i, 1), :] = own[pl.ds(last, 1), :]
            slab[pl.ds(rows + i, 1), :] = -own[pl.ds(rows + last, 1), :]
            slab[pl.ds(2 * rows + i, 1), :] = own[pl.ds(3 * rows + last, 1), :]
            slab[pl.ds(3 * rows + i, 1), :] = -own[pl.ds(2 * rows + last - 1, 1), :]
        slab[pl.ds(3 * rows + 12, 1), :] = -own[pl.ds(3 * rows - 1, 1), :]

    pl.semaphore_wait(barrier, len(peers) + jnp.where(ring, GROUP - jnp.where(keeper, 1, 0) + jnp.where(has_next, 1, 0), 0))

    pivot_col = lax.rem(fold[0] + lon * cols, n_lon * cols)
    q = lax.div(pivot_col, cols)
    r = lax.rem(pivot_col, cols)

    def halo_copy(side):
        d_lat, d_lon = STEP[side]
        slot = OPPOSITE[side]
        if d_lon == 0:
            src, dst = own, halo.at[0 if slot == N else 1]
        else:
            src, dst = side_out.at[0 if d_lon == 1 else 1], side_in.at[slot]
        return remote(
            src,
            dst,
            halo_send.at[side],
            halo_recv.at[slot],
            {"lat": lat_at(d_lat), "lon": lon_at(d_lon)},
        )

    def halo_wait(side):
        dst = halo.at[0 if side == N else 1] if side in (N, S) else side_in.at[side]
        remote(dst, dst, halo_send.at[side], halo_recv.at[side], {"lon": lon}).wait_recv()

    for side in (E, W):
        halo_copy(side).start()

    @pl.when(jnp.logical_not(top))
    def _():
        for side in (N, NE, NW):
            halo_copy(side).start()

    @pl.when(jnp.logical_not(bottom))
    def _():
        for side in (S, SE, SW):
            halo_copy(side).start()

    def hold_copy(size):
        slot = lon >> 2
        return remote(
            slab.at[pl.ds(0, size)],
            hold.at[slot, pl.ds(0, size)],
            hold_send.at[0],
            hold_recv.at[slot],
            {"lon": partner(0)},
        )

    def wanted(kind, to):
        low = q - to - 2 + 2 * n_lon
        return (low + ((kind - low) & (GROUP - 1))) & (n_lon - 1)

    def kind_of(place):
        return jnp.where(keeper, GROUP - 1 - place, place)

    def lowest(kind, g):
        return wanted(kind, g * GROUP + GROUP - 1) >> 2

    @pl.when(top)
    def _():
        hold_copy(4 * rows).start()

    for copy in large:
        copy.wait()
    u_base = 0
    v_base = depth * rows
    edge_lat[0, pl.ds(0, depth), :] = tr[pl.ds(rows - 1, depth, stride=rows), :]
    edge_lat[0, pl.ds(depth, depth), :] = vel[pl.ds(v_base + rows - 1, depth, stride=rows), :]
    edge_lat[1, pl.ds(0, depth), :] = tr[pl.ds(0, depth, stride=rows), :]
    edge_lat[1, pl.ds(depth, depth), :] = vel[pl.ds(v_base, depth, stride=rows), :]

    def spread_copy(j):
        to = (t_relay, v_relay)[j]
        return remote(
            edge_lat.at[0, pl.ds(j * depth, depth)],
            slab.at[pl.ds(0, depth)],
            trac_send.at[j],
            trac_recv.at[4],
            {"lat": to},
        )

    def lat_copy(north):
        slot = 1 if north else 0
        return remote(
            edge_lat.at[0 if north else 1],
            halo_lat.at[slot],
            trac_send.at[0 if north else 2],
            trac_recv.at[slot],
            {"lat": lat_at(1 if north else -1)},
        )

    @pl.when(top)
    def _():
        spread_copy(0).start()
        spread_copy(1).start()

    @pl.when(jnp.logical_not(top))
    def _():
        lat_copy(True).start()

    @pl.when(jnp.logical_not(bottom))
    def _():
        lat_copy(False).start()

    half = lane8 >> 1

    def pack(l, carry):
        pt, pu = carry
        for g in range(2):
            item = l + depth * g
            here = half == jnp.full((8, cols), item, jnp.int32)
            at = pl.multiple_of(l * rows + 8 * g, 8)
            pt = jnp.where(here, pltpu.roll(tr[pl.ds(at, 8), :], 2 * item + 1, axis=1), pt)
            pu = jnp.where(here, pltpu.roll(vel[pl.ds(at, 8), :], 2 * item + 1, axis=1), pu)
        return pt, pu

    pt, pu = lax.fori_loop(
        0, depth, pack, (jnp.zeros((8, cols), jnp.float32), jnp.zeros((8, cols), jnp.float32)), unroll=4
    )
    edge_lon[pl.ds(0, 8), :] = pt
    edge_lon[pl.ds(8, 8), :] = pu

    def lon_copy(east):
        slot = 1 if east else 0
        return remote(
            edge_lon,
            halo_lon.at[slot],
            trac_send.at[3 if east else 4],
            trac_recv.at[2 + slot],
            {"lon": lon_at(1 if east else -1)},
        )

    lon_copy(True).start()
    lon_copy(False).start()


    def trac_wait(dst, sem):
        remote(dst, dst, trac_send.at[5], sem, {"lon": lon}).wait_recv()

    @pl.when(relay)
    def _():
        trac_wait(slab.at[pl.ds(0, depth)], trac_recv.at[4])
        hold_copy(depth).start()

    h_own = own[pl.ds(3 * rows, rows), :]

    def pivots(l, carry):
        c_up, p_up = carry
        wet_below = (jnp.full((rows, cols), (l + 1).astype(jnp.float32)) < h_own).astype(jnp.float32)
        c_down = vert[jnp.minimum(l, depth - 2)] * wet_below
        pivot = (1.0 + c_up + c_down) + c_up * p_up
        inv = 1.0 / pivot
        p_down = -c_down * inv
        at = pl.ds(pl.multiple_of(l * rows, rows), rows)
        cpl[at, :] = c_up
        rec[at, :] = inv
        prime[at, :] = p_down
        mix_rows[pl.ds(l, 1), :] = jnp.full((1, cols), horiz[l])
        return c_down, p_down

    zero = jnp.zeros((rows, cols), jnp.float32)
    lax.fori_loop(0, depth, pivots, (zero, zero), unroll=2)

    lane16 = lax.broadcasted_iota(jnp.int32, (rows, cols), 1)
    row16 = lax.broadcasted_iota(jnp.int32, (rows, cols), 0)
    last_col = lane16 == cols - 1
    first_col = lane16 == 0
    last_row = row16 == rows - 1
    first_row = row16 == 0
    h_e = jnp.where(last_col, 0.0, pltpu.roll(h_own, cols - 1, axis=1))
    h_n = jnp.where(last_row, 0.0, pltpu.roll(h_own, rows - 1, axis=0))

    def fluxes(l, carry):
        at = pl.ds(pl.multiple_of(l * rows, rows), rows)
        t = tr[at, :]
        u = vel[at, :]
        v = vel[pl.ds(pl.multiple_of(v_base + l * rows, rows), rows), :]
        m = horiz[l]
        level = jnp.full((rows, cols), l.astype(jnp.float32))
        wet = (level < h_own).astype(jnp.float32)
        wet_e = (level < h_e).astype(jnp.float32)
        wet_n = (level < h_n).astype(jnp.float32)
        t_e = pltpu.roll(t, cols - 1, axis=1)
        u_e = pltpu.roll(u, cols - 1, axis=1)
        f_e = wet * wet_e * (m * (t_e - t) - 0.25 * (u + u_e) * (t + t_e))
        f_w = pltpu.roll(f_e, 1, axis=1)
        t_n = pltpu.roll(t, rows - 1, axis=0)
        v_n = pltpu.roll(v, rows - 1, axis=0)
        f_n = wet * wet_n * (m * (t_n - t) - 0.25 * (v + v_n) * (t + t_n))
        f_s = pltpu.roll(f_n, 1, axis=0)
        step_ref[at, :] = wet * (t + ((f_e - f_w) + (f_n - f_s)))
        return carry

    lax.fori_loop(0, depth, fluxes, 0, unroll=4)

    def final_copy(e, size, dst, recv):
        return remote(
            pick.at[e, pl.ds(0, size)], dst, fin_send.at[e], recv, {"lat": n_lat - 1, "lon": group + e}
        )

    def forward_copy(out, slot, to, size):
        return remote(
            fwd_out.at[out, pl.ds(0, size)], fwd_in.at[slot, pl.ds(0, size)], fwd_send.at[out], fwd_recv.at[slot], {"lon": to}
        )

    def chain_copy(slot, size):
        return remote(
            fwd_in.at[slot, pl.ds(0, size)],
            fwd_in.at[slot - 1, pl.ds(0, size)],
            fwd_send.at[slot],
            fwd_recv.at[slot - 1],
            {"lon": lon + onward},
        )

    def chain_wait(slot, size):
        dst = fwd_in.at[slot, pl.ds(0, size)]
        remote(dst, dst, fwd_send.at[0], fwd_recv.at[slot], {"lon": partner(0)}).wait_recv()

    rise, fall = half_way + 1, half_way

    def serve(size, block, target):
        def send(e, carry):
            pick[e, pl.ds(0, size), :] = block(e)
            target(e)
            return carry

        lax.fori_loop(0, GROUP, send, 0)

    def to_top(e):
        @pl.when(e != me)
        def _():
            final_copy(e, 4 * rows, fin.at[me], fin_recv.at[me]).start()

    def to_relayed(j):
        return lambda e: final_copy(e, depth, tfin.at[j, me], tfin_recv.at[j, me]).start()

    members = ((top, 4 * rows, to_top), (is_t_relay, depth, to_relayed(0)), (is_v_relay, depth, to_relayed(1)))

    for role, size, target in members:

        @pl.when(role & keeper)
        def _(size=size, target=target):
            for g in range(n_group):
                dst = hold.at[g, pl.ds(0, size)]
                remote(dst, dst, hold_send.at[0], hold_recv.at[g], {"lon": partner(0)}).wait_recv()
            serve(size, lambda e: hold[wanted(GROUP - 1 - me, e) >> 2, pl.ds(0, size), :], target)

            first_up = lowest(GROUP - 1 - me, 1)
            first_down = lowest(GROUP - 1 - me, n_group - 1)

            def forward_up(j, carry):
                slot = (first_up + 1 - j + n_group) & (n_group - 1)
                fwd_out[j, pl.ds(0, size), :] = hold[slot, pl.ds(0, size), :]
                forward_copy(j, j, partner(1), size).start()
                return carry

            def forward_down(j, carry):
                slot = (first_down + j) & (n_group - 1)
                fwd_out[rise + j, pl.ds(0, size), :] = hold[slot, pl.ds(0, size), :]
                forward_copy(rise + j, j, partner(n_group - 1), size).start()
                return carry

            lax.fori_loop(0, rise, forward_up, 0)
            lax.fori_loop(0, fall, forward_down, 0)

    for side in (E, W):
        halo_wait(side)

    @pl.when(jnp.logical_not(top))
    def _():
        for side in (N, NE, NW):
            halo_wait(side)

    @pl.when(jnp.logical_not(bottom))
    def _():
        for side in (S, SE, SW):
            halo_wait(side)

    near = lane8 < cols // 2
    west_half, east_half = pl.ds(0, cols), pl.ds(cols, cols)

    def beside(east, west, base):
        for k in range(8):
            tile = jnp.where(
                near,
                pltpu.roll(side_in[east], (cols - 16 * k) % cols, axis=1),
                pltpu.roll(side_in[west], (cols - 16 - 16 * k) % cols, axis=1),
            )
            ext[k // 2, pl.ds(base + 8 * (k % 2), 8), east_half] = tile

    beside(SE, SW, 0)
    beside(E, W, rows)
    for f in range(4):
        part = pl.ds(f * rows, rows)
        ext[f, pl.ds(0, rows), west_half] = halo[1, part, :]
        ext[f, pl.ds(rows, rows), west_half] = own[part, :]
    fold_fix[...] = jnp.zeros((8, 2 * cols), jnp.float32)

    @pl.when(jnp.logical_not(top))
    def _():
        beside(NE, NW, 2 * rows)
        for f in range(4):
            ext[f, pl.ds(2 * rows, rows), west_half] = halo[0, pl.ds(f * rows, rows), :]

    trac_wait(halo_lon.at[0], trac_recv.at[2])
    trac_wait(halo_lon.at[1], trac_recv.at[3])

    @pl.when(jnp.logical_not(top))
    def _():
        trac_wait(halo_lat.at[0], trac_recv.at[0])

    @pl.when(jnp.logical_not(bottom))
    def _():
        trac_wait(halo_lat.at[1], trac_recv.at[1])

    even = (lane8 & 1) == 0
    h_beside = ext[3, pl.ds(rows, rows), east_half]
    h_north_row = halo[0, pl.ds(3 * rows, 1), :]
    h_south_row = halo[1, pl.ds(4 * rows - 1, 1), :]

    def swap(from_east, from_west):
        return jnp.where(
            even, pltpu.roll(from_east, cols - 1, axis=1), pltpu.roll(from_west, 1, axis=1)
        )

    pt = edge_lon[pl.ds(0, 8), :]
    pu = edge_lon[pl.ds(8, 8), :]
    th = swap(halo_lon[0, pl.ds(0, 8), :], halo_lon[1, pl.ds(0, 8), :])
    uh = swap(halo_lon[0, pl.ds(8, 8), :], halo_lon[1, pl.ds(8, 8), :])

    def column(tile, at):
        lo = jnp.broadcast_to(tile[0:8, at : at + 1], (8, cols))
        hi = jnp.broadcast_to(tile[8:16, at : at + 1], (8, cols))
        return jnp.where(half < depth, lo, hi)

    level_of = (half & (depth - 1)).astype(jnp.float32)
    h_in = jnp.where(even, column(h_own, cols - 1), column(h_own, 0))
    h_out = jnp.where(even, column(h_beside, 0), column(h_beside, cols - 1))
    wet_pair = (level_of < h_in).astype(jnp.float32) * (level_of < h_out).astype(jnp.float32)

    def lane_mix(l, acc):
        return jnp.where((half & (depth - 1)) == jnp.full((8, cols), l, jnp.int32), horiz[l], acc)

    mix_lanes = lax.fori_loop(0, depth, lane_mix, jnp.zeros((8, cols), jnp.float32), unroll=4)
    sign = jnp.where(even, 1.0, -1.0)
    side_flux = wet_pair * (mix_lanes * (th - pt) - sign * (0.25 * (pu + uh) * (pt + th)))

    level_row = lax.broadcasted_iota(jnp.int32, (depth, cols), 0).astype(jnp.float32)

    def row_face(low_t, low_v, high_t, high_v, h_low, h_high):
        wet = (level_row < h_low).astype(jnp.float32) * (level_row < h_high).astype(jnp.float32)
        return wet * (mix_rows[...] * (high_t - low_t) - 0.25 * (low_v + high_v) * (low_t + high_t))

    first, second = pl.ds(0, depth), pl.ds(depth, depth)
    face_lat[0] = row_face(
        edge_lat[0, first, :], edge_lat[0, second, :], halo_lat[0, first, :], halo_lat[0, second, :],
        own[pl.ds(4 * rows - 1, 1), :], h_north_row,
    )
    face_lat[1] = row_face(
        halo_lat[1, first, :], halo_lat[1, second, :], edge_lat[1, first, :], edge_lat[1, second, :],
        h_south_row, own[pl.ds(3 * rows, 1), :],
    )

    rim_col = last_col | first_col

    def forward(l, sweep):
        at = pl.ds(pl.multiple_of(l * rows, rows), rows)
        rim = jnp.concatenate(
            [
                pltpu.roll(side_flux, cols - 1 - 2 * l, axis=1),
                pltpu.roll(side_flux, lax.rem(2 * cols - 1 - 2 * (l + depth), cols), axis=1),
            ],
            axis=0,
        )
        gain = jnp.where(rim_col, rim, 0.0) + (
            jnp.where(last_row, face_lat[0, pl.ds(l, 1), :], 0.0)
            - jnp.where(first_row, face_lat[1, pl.ds(l, 1), :], 0.0)
        )
        sweep = ((step_ref[at, :] + gain) + cpl[at, :] * sweep) * rec[at, :]
        step_ref[at, :] = sweep
        return sweep

    lax.fori_loop(0, depth, forward, zero, unroll=4)

    def backward(i, x):
        l = depth - 1 - i
        at = pl.ds(pl.multiple_of(l * rows, rows), rows)
        x = step_ref[at, :] - prime[at, :] * x
        tracer_out[at, :] = x
        return x

    lax.fori_loop(0, depth, backward, zero, unroll=4)

    for role, size, target in members:

        @pl.when(role & jnp.logical_not(keeper))
        def _(size=size, target=target):
            chain_wait(0, size)
            chain_wait(1, size)

            @pl.when(has_next)
            def _():
                chain_copy(1, size).start()

            first_slot = lowest(me, at_group)
            turned = jnp.where(rising, 1, 0)

            def either(e):
                which = ((wanted(me, group + e) >> 2) - first_slot + turned) & 1
                return jnp.where(
                    jnp.full((size, cols), which, jnp.int32) == 1,
                    fwd_in[1, pl.ds(0, size), :],
                    fwd_in[0, pl.ds(0, size), :],
                )

            serve(size, either, target)

            def hand_on(slot, carry):
                chain_wait(slot, size)
                chain_copy(slot, size).start()
                return carry

            lax.fori_loop(2, blocks, hand_on, 0)

    def source_of(shape, shift, isu):
        s = lax.broadcasted_iota(jnp.int32, shape, 1)
        l = (jnp.full(shape, r, jnp.int32) - isu - s) & (cols - 1)
        return s, l

    @pl.when(top)
    def _():
        shape = (4 * rows, cols)
        row = lax.broadcasted_iota(jnp.int32, shape, 0)
        isu = ((row >= rows) & (row < 2 * rows)).astype(jnp.int32)
        s, l = source_of(shape, 0, isu)
        whole = n_lon * cols
        base = jnp.full(shape, pivot_col - lon * cols + 2 * whole, jnp.int32) - isu
        dev_main = ((base - l) & (whole - 1)) >> 7
        off = jnp.where(l < cols // 2, cols, -cols)
        dev_side = ((base - l - off) & (whole - 1)) >> 7
        main, side = zeros_tile, zeros_tile
        for e in range(GROUP):
            @pl.when(e != me)
            def _():
                trac_wait(fin.at[e], fin_recv.at[e])

            @pl.when(e == me)
            def _():
                fin[e] = pick[e]

        for e in range(GROUP):
            got = fin[e]
            src = jnp.full(shape, wanted(kind_of(e), lon), jnp.int32)
            main = jnp.where(dev_main == src, got, main)
            side = jnp.where(dev_side == src, got, side)
        main = jnp.take_along_axis(main, l, axis=1)
        side = jnp.take_along_axis(side, l, axis=1)
        for f in range(4):
            ff = (0, 1, 3, 2)[f]
            ext[ff, pl.ds(2 * rows, rows), west_half] = main[f * rows : (f + 1) * rows]
            ext[ff, pl.ds(2 * rows, rows), east_half] = side[f * rows : (f + 1) * rows]
        fold_fix[pl.ds(0, 1), west_half] = main[3 * rows + 12 : 3 * rows + 13] - ext[2, pl.ds(2 * rows - 1, 1), west_half]
        fold_fix[pl.ds(0, 1), east_half] = side[3 * rows + 12 : 3 * rows + 13] - ext[2, pl.ds(2 * rows - 1, 1), east_half]

    wide = 2 * cols
    tall = 3 * rows
    h = ext[3]
    sea = (h > 0.0).astype(jnp.float32)

    def east(x):
        return pltpu.roll(x, wide - 1, axis=1)

    def north(x):
        return pltpu.roll(x, tall - 1, axis=0)

    zonal_mask = sea * east(sea)
    merid_mask = sea * north(sea)
    coef[0] = fb_step * ((h + east(h)) / (2.0 * depth)) * zonal_mask
    coef[1] = (1.0 - drag_rate) * zonal_mask
    coef[2] = fb_step * ((h + north(h)) / (2.0 * depth)) * merid_mask
    coef[3] = (1.0 - drag_rate) * merid_mask
    coef[4] = fb_step * sea
    fix_decay = pltpu.roll(coef[3], 1, axis=0)[2 * rows : 2 * rows + 8]

    def cycle(i, state):
        eta, u, v, fix = state
        v_south = pltpu.roll(v, 1, axis=0)
        v_south = jnp.concatenate(
            [v_south[: 2 * rows], v_south[2 * rows : 2 * rows + 8] + fix, v_south[2 * rows + 8 :]], axis=0
        )
        div = (u - pltpu.roll(u, 1, axis=1)) + (v - v_south)
        eta = eta - coef[4] * div
        u = u * coef[1] - coef[0] * (east(eta) - eta)
        v = v * coef[3] - coef[2] * (north(eta) - eta)
        return eta, u, v, fix * fix_decay

    eta, u, v, _ = lax.fori_loop(0, SUB, cycle, (ext[0] * sea, ext[1], ext[2], fold_fix[...]))
    surface_out[...] = eta[rows : 2 * rows, :cols]
    transport_out[pl.ds(0, rows), :] = u[rows : 2 * rows, :cols]
    transport_out[pl.ds(rows, rows), :] = v[rows : 2 * rows, :cols]

    @pl.when(top)
    def _():
        got = []
        for j in range(2):
            shape = (depth, cols)
            s, l = source_of(shape, 0, 0)
            whole = n_lon * cols
            dev = ((jnp.full(shape, pivot_col - lon * cols + 2 * whole, jnp.int32) - l) & (whole - 1)) >> 7
            acc = jnp.zeros(shape, jnp.float32)
            for e in range(GROUP):
                trac_wait(tfin.at[j, e], tfin_recv.at[j, e])
                acc = jnp.where(dev == jnp.full(shape, wanted(kind_of(e), lon), jnp.int32), tfin[j, e], acc)
            got.append(jnp.take_along_axis(acc, l, axis=1))
        h_last = own[pl.ds(4 * rows - 1, 1), :]
        flux = row_face(
            edge_lat[0, first, :], edge_lat[0, second, :], got[0], got[1], h_last, ext[3, pl.ds(2 * rows, 1), west_half]
        )
        face_lat[0] = (level_row < h_last).astype(jnp.float32) * flux
        c_last = cpl[pl.ds(rows - 1, depth, stride=rows), :]
        r_last = rec[pl.ds(rows - 1, depth, stride=rows), :]
        p_last = prime[pl.ds(rows - 1, depth, stride=rows), :]
        out_last = tracer_out[pl.ds(rows - 1, depth, stride=rows), :]
        delta = face_lat[0]
        sweeps = []
        x = jnp.zeros((1, cols), jnp.float32)
        for k in range(depth):
            x = (delta[k : k + 1] + c_last[k : k + 1] * x) * r_last[k : k + 1]
            sweeps.append(x)
        x = jnp.zeros((1, cols), jnp.float32)
        for k in range(depth - 1, -1, -1):
            x = sweeps[k] - p_last[k : k + 1] * x
            tracer_out[pl.ds(k * rows + rows - 1, 1), :] = out_last[k : k + 1] + x

    for side in (E, W):
        halo_copy(side).wait_send()
    lon_copy(True).wait_send()
    lon_copy(False).wait_send()

    @pl.when(jnp.logical_not(top))
    def _():
        for side in (N, NE, NW):
            halo_copy(side).wait_send()
        lat_copy(True).wait_send()

    @pl.when(jnp.logical_not(bottom))
    def _():
        for side in (S, SE, SW):
            halo_copy(side).wait_send()
        lat_copy(False).wait_send()

    @pl.when(top)
    def _():
        spread_copy(0).wait_send()
        spread_copy(1).wait_send()

        hold_copy(4 * rows).wait_send()

        @pl.when(keeper)
        def _():
            for j in range(rise):
                forward_copy(j, j, partner(1), 4 * rows).wait_send()
            for j in range(fall):
                forward_copy(rise + j, j, partner(n_group - 1), 4 * rows).wait_send()

        @pl.when(has_next)
        def _():
            def gone(slot, carry):
                chain_copy(slot, 4 * rows).wait_send()
                return carry

            lax.fori_loop(1, blocks, gone, 0)

        for e in range(GROUP):

            @pl.when(e != me)
            def _(e=e):
                final_copy(e, 4 * rows, fin.at[me], fin_recv.at[me]).wait_send()

    @pl.when(relay)
    def _():
        hold_copy(depth).wait_send()

        @pl.when(keeper)
        def _():
            for j in range(rise):
                forward_copy(j, j, partner(1), depth).wait_send()
            for j in range(fall):
                forward_copy(rise + j, j, partner(n_group - 1), depth).wait_send()

        @pl.when(has_next)
        def _():
            def gone(slot, carry):
                chain_copy(slot, depth).wait_send()
                return carry

            lax.fori_loop(1, blocks, gone, 0)

        for e in range(GROUP):
            final_copy(e, depth, tfin.at[0, me], tfin_recv.at[0, me]).wait_send()


def solution(mesh):
    n_lon, n_lat = mesh.shape["lon"], mesh.shape["lat"]

    def shards(tracer, velocity, surface, transport, horiz_mixing, vert_mixing, levels, land_tiles, fold_pair):
        depth, rows, cols = tracer.shape
        f32 = jnp.float32
        hbm = pl.BlockSpec(memory_space=pl.ANY)
        vmem = pl.BlockSpec(memory_space=pltpu.VMEM)
        dma = pltpu.SemaphoreType.DMA
        field = pltpu.VMEM((depth * rows, cols), f32)
        tracer_new, surface_new, transport_new = pl.pallas_call(
            functools.partial(ocean_kernel, n_lon, n_lat, depth, rows, cols),
            name="ocean",
            out_shape=(
                pltpu.VMEM((depth * rows, cols), f32),
                pltpu.VMEM((rows, cols), f32),
                pltpu.VMEM((2 * rows, cols), f32),
            ),
            in_specs=[hbm] * 9,
            out_specs=(vmem, vmem, vmem),
            scratch_shapes=[
                pltpu.SMEM((depth,), f32),
                pltpu.SMEM((depth - 1,), f32),
                pltpu.SMEM((1, 1), jnp.int32),
                pltpu.SMEM((cols,), jnp.int32),
                field,
                pltpu.VMEM((2 * depth * rows, cols), f32),
                pltpu.VMEM((rows, cols), jnp.int32),
                pltpu.VMEM((4 * rows, cols), f32),
                pltpu.VMEM((2, 4 * rows, cols), f32),
                pltpu.VMEM((2, 8, cols), f32),
                pltpu.VMEM((8, 8, cols), f32),
                pltpu.VMEM((16, cols), f32),
                pltpu.VMEM((2, 16, cols), f32),
                pltpu.VMEM((2, 2 * depth, cols), f32),
                pltpu.VMEM((2, 2 * depth, cols), f32),
                pltpu.VMEM((4 * rows, cols), f32),
                pltpu.VMEM((n_lon // GROUP, 4 * rows, cols), f32),
                pltpu.VMEM((n_lon // GROUP + 1, 4 * rows, cols), f32),
                pltpu.VMEM((n_lon // GROUP // 2 + 1, 4 * rows, cols), f32),
                pltpu.VMEM((GROUP, 4 * rows, cols), f32),
                pltpu.VMEM((GROUP, 4 * rows, cols), f32),
                pltpu.VMEM((2, GROUP, depth, cols), f32),
                field,
                field,
                field,
                field,
                pltpu.VMEM((2, depth, cols), f32),
                pltpu.VMEM((depth, cols), f32),
                pltpu.VMEM((4, 3 * rows, 2 * cols), f32),
                pltpu.VMEM((5, 3 * rows, 2 * cols), f32),
                pltpu.VMEM((8, 2 * cols), f32),
                dma((9,)),
                dma((8,)),
                dma((8,)),
                dma((6,)),
                dma((5,)),
                dma((1,)),
                dma((n_lon // GROUP,)),
                dma((n_lon // GROUP + 1,)),
                dma((n_lon // GROUP // 2 + 1,)),
                dma((GROUP,)),
                dma((GROUP,)),
                dma((2, GROUP)),
            ],
            compiler_params=pltpu.CompilerParams(collective_id=1, has_side_effects=True),
        )(
            tracer.reshape(depth * rows, cols),
            velocity.reshape(2 * depth * rows, cols),
            surface,
            transport.reshape(2 * rows, cols),
            levels,
            horiz_mixing,
            vert_mixing,
            land_tiles,
            fold_pair,
        )
        return (
            tracer_new.reshape(depth, rows, cols),
            surface_new,
            transport_new.reshape(2, rows, cols),
        )

    return jax.shard_map(
        shards,
        mesh=mesh,
        in_specs=(
            P("member", "lat", "lon"),
            P(None, "member", "lat", "lon"),
            P(("member", "lat"), "lon"),
            P("member", "lat", "lon"),
            P("member"),
            P("member"),
            P("lat", "lon"),
            P("lat", "lon"),
            P("lon"),
        ),
        out_specs=(
            P("member", "lat", "lon"),
            P(("member", "lat"), "lon"),
            P("member", "lat", "lon"),
        ),
        check_vma=False,
    )
```

time: 72.6 us -> 60.9 us (0.84)
  Pallas kernels: 68 us -> 57.4 us
  local copies, waits for them, and re-layouts: 3.01 us -> 1.91 us
    pallas_call x1, Pallas kernels: 68 us -> 57.4 us  [shards(): pl.pallas_call(functools.partial(ocean_kernel, n_lon, n_lat, depth, rows,...]
    unnamed x7 -> x3, local copies, waits for them, and re-layouts: 3.01 us -> 1.91 us
where the time goes in v2:
time: 60.9 us; the launch traced here: 60.6 us
  Pallas kernels  57.4 us (94%)
  local copies, waits for them, and re-layouts  1.91 us (3%)
  between operations  1.29 us (2%)
    pallas_call x1, Pallas kernels, shards(): pl.pallas_call(functools.partial(ocean_kernel, n_lon, n_lat, depth, rows,...  57.4 us
    unnamed x3, local copies, waits for them, and re-layouts  1.91 us

profile of v2, /device:TPU:39, one launch (start us, length us, event | category | flops | bytes accessed | tf_op | source)
XLA Modules:
  0.0 60.6 jit_solution(15824673940707247716)
XLA Ops:
  1.3 57.4 %ocean.1 = (f32[512,128]{1,0:T(8,128)S(1)}, f32[16,128]{1,0:T(8,128)S(1)}, f32[32,128]{1,0:T(8,128)S(1)}) custom-call(f32[512,128]{1,0:T(8,128)} %bitcast.8, f32[1024,128]{1,0:T(8,128)} %bitcast.7, f32[16,128]{1,0:T(8,128)} %surface_hbm.1, f32[32,128]{1,0:T(8,128)} %bitcast.9, s32[16,128]{1,0:T(8,128)} %levels_hbm.1, f32[32]{0:T(128)} %horiz_hbm.1, ...), custom_call_target="tpu_custom_call" | custom-call | tf_op jit(solution)/shard_map/ocean/pallas_call | solution.py:814
  58.7 0.7 %copy.15 = f32[32,16,128]{2,1,0:T(8,128)} copy(f32[32,16,128]{2,1,0:T(8,128)S(1)} %bitcast.5) | data formatting | bytes 524288
  59.4 0.6 copy.16
  60.0 0.6 copy.17

commit v3 on v2

--- a/solution.py
+++ b/solution.py
@@ -94,6 +94,7 @@
     me = lon & (GROUP - 1)
     group = lon - me
     keeper = lon < GROUP
+    block = 4 * SUB + 8
     half_way = n_group // 2
     at_group = lon >> 2
     rising = at_group <= half_way
@@ -190,14 +191,13 @@
 
     @pl.when(top)
     def _():
-        slab[...] = zeros_tile
-        for i in range(12):
-            last = rows - 1 - i
-            slab[pl.ds(i, 1), :] = own[pl.ds(last, 1), :]
-            slab[pl.ds(rows + i, 1), :] = -own[pl.ds(rows + last, 1), :]
-            slab[pl.ds(2 * rows + i, 1), :] = own[pl.ds(3 * rows + last, 1), :]
-            slab[pl.ds(3 * rows + i, 1), :] = -own[pl.ds(2 * rows + last - 1, 1), :]
-        slab[pl.ds(3 * rows + 12, 1), :] = -own[pl.ds(3 * rows - 1, 1), :]
+        slab[pl.ds(block - 8, 8), :] = jnp.zeros((8, cols), jnp.float32)
+        for f, (start, back, sign) in enumerate(((0, 0, 1), (rows, 0, -1), (3 * rows, 0, 1), (2 * rows, 1, -1))):
+            for i in range(SUB):
+                row = own[pl.ds(start + rows - 1 - i - back, 1), :]
+                at = 8 * f + i if i < 8 else 32 + (SUB - 8) * f + i - 8
+                slab[pl.ds(at, 1), :] = row if sign == 1 else -row
+        slab[pl.ds(block - 8, 1), :] = -own[pl.ds(3 * rows - 1, 1), :]
 
     pl.semaphore_wait(barrier, len(peers) + jnp.where(ring, GROUP - jnp.where(keeper, 1, 0) + jnp.where(has_next, 1, 0), 0))
 
@@ -259,7 +259,7 @@
 
     @pl.when(top)
     def _():
-        hold_copy(4 * rows).start()
+        hold_copy(block).start()
 
     for copy in large:
         copy.wait()
@@ -430,12 +430,12 @@
     def to_top(e):
         @pl.when(e != me)
         def _():
-            final_copy(e, 4 * rows, fin.at[me], fin_recv.at[me]).start()
+            final_copy(e, block, fin.at[me], fin_recv.at[me]).start()
 
     def to_relayed(j):
         return lambda e: final_copy(e, depth, tfin.at[j, me], tfin_recv.at[j, me]).start()
 
-    members = ((top, 4 * rows, to_top), (is_t_relay, depth, to_relayed(0)), (is_v_relay, depth, to_relayed(1)))
+    members = ((top, block, to_top), (is_t_relay, depth, to_relayed(0)), (is_v_relay, depth, to_relayed(1)))
 
     for role, size, target in members:
 
@@ -480,28 +480,31 @@
     near = lane8 < cols // 2
     west_half, east_half = pl.ds(0, cols), pl.ds(cols, cols)
 
-    def beside(east, west, base):
+    low, high = SUB, SUB + rows
+
+    def beside(east, west, base, first, last):
         for k in range(8):
             tile = jnp.where(
                 near,
                 pltpu.roll(side_in[east], (cols - 16 * k) % cols, axis=1),
                 pltpu.roll(side_in[west], (cols - 16 - 16 * k) % cols, axis=1),
             )
-            ext[k // 2, pl.ds(base + 8 * (k % 2), 8), east_half] = tile
-
-    beside(SE, SW, 0)
-    beside(E, W, rows)
+            at = 8 * (k % 2)
+            lo, hi = max(first, at), min(last, at + 8)
+            ext[k // 2, pl.ds(base + lo - first, hi - lo), east_half] = tile[lo - at : hi - at]
+
+    beside(SE, SW, 0, rows - SUB, rows)
+    beside(E, W, low, 0, rows)
     for f in range(4):
-        part = pl.ds(f * rows, rows)
-        ext[f, pl.ds(0, rows), west_half] = halo[1, part, :]
-        ext[f, pl.ds(rows, rows), west_half] = own[part, :]
+        ext[f, pl.ds(0, SUB), west_half] = halo[1, pl.ds((f + 1) * rows - SUB, SUB), :]
+        ext[f, pl.ds(low, rows), west_half] = own[pl.ds(f * rows, rows), :]
     fold_fix[...] = jnp.zeros((8, 2 * cols), jnp.float32)
 
     @pl.when(jnp.logical_not(top))
     def _():
-        beside(NE, NW, 2 * rows)
+        beside(NE, NW, high, 0, SUB)
         for f in range(4):
-            ext[f, pl.ds(2 * rows, rows), west_half] = halo[0, pl.ds(f * rows, rows), :]
+            ext[f, pl.ds(high, SUB), west_half] = halo[0, pl.ds(f * rows, SUB), :]
 
     trac_wait(halo_lon.at[0], trac_recv.at[2])
     trac_wait(halo_lon.at[1], trac_recv.at[3])
@@ -515,7 +518,7 @@
         trac_wait(halo_lat.at[1], trac_recv.at[1])
 
     even = (lane8 & 1) == 0
-    h_beside = ext[3, pl.ds(rows, rows), east_half]
+    h_beside = ext[3, pl.ds(low, rows), east_half]
     h_north_row = halo[0, pl.ds(3 * rows, 1), :]
     h_south_row = halo[1, pl.ds(4 * rows - 1, 1), :]
 
@@ -630,16 +633,17 @@
 
     @pl.when(top)
     def _():
-        shape = (4 * rows, cols)
+        shape = (block, cols)
         row = lax.broadcasted_iota(jnp.int32, shape, 0)
-        isu = ((row >= rows) & (row < 2 * rows)).astype(jnp.int32)
+        isu = (((row >= 8) & (row < 16)) | ((row >= 24 + SUB) & (row < 16 + 2 * SUB))).astype(jnp.int32)
         s, l = source_of(shape, 0, isu)
         whole = n_lon * cols
         base = jnp.full(shape, pivot_col - lon * cols + 2 * whole, jnp.int32) - isu
         dev_main = ((base - l) & (whole - 1)) >> 7
         off = jnp.where(l < cols // 2, cols, -cols)
         dev_side = ((base - l - off) & (whole - 1)) >> 7
-        main, side = zeros_tile, zeros_tile
+        main = jnp.zeros(shape, jnp.float32)
+        side = main
         for e in range(GROUP):
             @pl.when(e != me)
             def _():
@@ -658,13 +662,15 @@
         side = jnp.take_along_axis(side, l, axis=1)
         for f in range(4):
             ff = (0, 1, 3, 2)[f]
-            ext[ff, pl.ds(2 * rows, rows), west_half] = main[f * rows : (f + 1) * rows]
-            ext[ff, pl.ds(2 * rows, rows), east_half] = side[f * rows : (f + 1) * rows]
-        fold_fix[pl.ds(0, 1), west_half] = main[3 * rows + 12 : 3 * rows + 13] - ext[2, pl.ds(2 * rows - 1, 1), west_half]
-        fold_fix[pl.ds(0, 1), east_half] = side[3 * rows + 12 : 3 * rows + 13] - ext[2, pl.ds(2 * rows - 1, 1), east_half]
+            rest = 32 + (SUB - 8) * f
+            for half_of, part in ((west_half, main), (east_half, side)):
+                ext[ff, pl.ds(high, 8), half_of] = part[8 * f : 8 * f + 8]
+                ext[ff, pl.ds(high + 8, SUB - 8), half_of] = part[rest : rest + SUB - 8]
+        for half_of, part in ((west_half, main), (east_half, side)):
+            fold_fix[pl.ds(high - 24, 1), half_of] = part[block - 8 : block - 7] - ext[2, pl.ds(high - 1, 1), half_of]
 
     wide = 2 * cols
-    tall = 3 * rows
+    tall = rows + 2 * SUB
     h = ext[3]
     sea = (h > 0.0).astype(jnp.float32)
 
@@ -681,13 +687,13 @@
     coef[2] = fb_step * ((h + north(h)) / (2.0 * depth)) * merid_mask
     coef[3] = (1.0 - drag_rate) * merid_mask
     coef[4] = fb_step * sea
-    fix_decay = pltpu.roll(coef[3], 1, axis=0)[2 * rows : 2 * rows + 8]
+    fix_decay = pltpu.roll(coef[3], 1, axis=0)[24:32]
 
     def cycle(i, state):
         eta, u, v, fix = state
         v_south = pltpu.roll(v, 1, axis=0)
         v_south = jnp.concatenate(
-            [v_south[: 2 * rows], v_south[2 * rows : 2 * rows + 8] + fix, v_south[2 * rows + 8 :]], axis=0
+            [v_south[:24], v_south[24:32] + fix, v_south[32:]], axis=0
         )
         div = (u - pltpu.roll(u, 1, axis=1)) + (v - v_south)
         eta = eta - coef[4] * div
@@ -696,9 +702,9 @@
         return eta, u, v, fix * fix_decay
 
     eta, u, v, _ = lax.fori_loop(0, SUB, cycle, (ext[0] * sea, ext[1], ext[2], fold_fix[...]))
-    surface_out[...] = eta[rows : 2 * rows, :cols]
-    transport_out[pl.ds(0, rows), :] = u[rows : 2 * rows, :cols]
-    transport_out[pl.ds(rows, rows), :] = v[rows : 2 * rows, :cols]
+    surface_out[...] = eta[low:high, :cols]
+    transport_out[pl.ds(0, rows), :] = u[low:high, :cols]
+    transport_out[pl.ds(rows, rows), :] = v[low:high, :cols]
 
     @pl.when(top)
     def _():
@@ -715,7 +721,7 @@
             got.append(jnp.take_along_axis(acc, l, axis=1))
         h_last = own[pl.ds(4 * rows - 1, 1), :]
         flux = row_face(
-            edge_lat[0, first, :], edge_lat[0, second, :], got[0], got[1], h_last, ext[3, pl.ds(2 * rows, 1), west_half]
+            edge_lat[0, first, :], edge_lat[0, second, :], got[0], got[1], h_last, ext[3, pl.ds(high, 1), west_half]
         )
         face_lat[0] = (level_row < h_last).astype(jnp.float32) * flux
         c_last = cpl[pl.ds(rows - 1, depth, stride=rows), :]
@@ -755,19 +761,19 @@
         spread_copy(0).wait_send()
         spread_copy(1).wait_send()
 
-        hold_copy(4 * rows).wait_send()
+        hold_copy(block).wait_send()
 
         @pl.when(keeper)
         def _():
             for j in range(rise):
-                forward_copy(j, j, partner(1), 4 * rows).wait_send()
+                forward_copy(j, j, partner(1), block).wait_send()
             for j in range(fall):
-                forward_copy(rise + j, j, partner(n_group - 1), 4 * rows).wait_send()
+                forward_copy(rise + j, j, partner(n_group - 1), block).wait_send()
 
         @pl.when(has_next)
         def _():
             def gone(slot, carry):
-                chain_copy(slot, 4 * rows).wait_send()
+                chain_copy(slot, block).wait_send()
                 return carry
 
             lax.fori_loop(1, blocks, gone, 0)
@@ -776,7 +782,7 @@
 
             @pl.when(e != me)
             def _(e=e):
-                final_copy(e, 4 * rows, fin.at[me], fin_recv.at[me]).wait_send()
+                final_copy(e, block, fin.at[me], fin_recv.at[me]).wait_send()
 
     @pl.when(relay)
     def _():
@@ -799,6 +805,17 @@
 
         for e in range(GROUP):
             final_copy(e, depth, tfin.at[0, me], tfin_recv.at[0, me]).wait_send()
+
+
+def write_out(a, b, c, a_hbm, b_hbm, c_hbm, sem):
+    copies = [
+        pltpu.make_async_copy(src, dst, sem.at[i])
+        for i, (src, dst) in enumerate(((a, a_hbm), (b, b_hbm), (c, c_hbm)))
+    ]
+    for copy in copies:
+        copy.start()
+    for copy in copies:
+        copy.wait()
 
 
 def solution(mesh):
@@ -811,7 +828,7 @@
         vmem = pl.BlockSpec(memory_space=pltpu.VMEM)
         dma = pltpu.SemaphoreType.DMA
         field = pltpu.VMEM((depth * rows, cols), f32)
-        tracer_new, surface_new, transport_new = pl.pallas_call(
+        results = pl.pallas_call(
             functools.partial(ocean_kernel, n_lon, n_lat, depth, rows, cols),
             name="ocean",
             out_shape=(
@@ -837,12 +854,12 @@
                 pltpu.VMEM((2, 16, cols), f32),
                 pltpu.VMEM((2, 2 * depth, cols), f32),
                 pltpu.VMEM((2, 2 * depth, cols), f32),
-                pltpu.VMEM((4 * rows, cols), f32),
-                pltpu.VMEM((n_lon // GROUP, 4 * rows, cols), f32),
-                pltpu.VMEM((n_lon // GROUP + 1, 4 * rows, cols), f32),
-                pltpu.VMEM((n_lon // GROUP // 2 + 1, 4 * rows, cols), f32),
-                pltpu.VMEM((GROUP, 4 * rows, cols), f32),
-                pltpu.VMEM((GROUP, 4 * rows, cols), f32),
+                pltpu.VMEM((4 * SUB + 8, cols), f32),
+                pltpu.VMEM((n_lon // GROUP, 4 * SUB + 8, cols), f32),
+                pltpu.VMEM((n_lon // GROUP + 1, 4 * SUB + 8, cols), f32),
+                pltpu.VMEM((n_lon // GROUP // 2 + 1, 4 * SUB + 8, cols), f32),
+                pltpu.VMEM((GROUP, 4 * SUB + 8, cols), f32),
+                pltpu.VMEM((GROUP, 4 * SUB + 8, cols), f32),
                 pltpu.VMEM((2, GROUP, depth, cols), f32),
                 field,
                 field,
@@ -850,8 +867,8 @@
                 field,
                 pltpu.VMEM((2, depth, cols), f32),
                 pltpu.VMEM((depth, cols), f32),
-                pltpu.VMEM((4, 3 * rows, 2 * cols), f32),
-                pltpu.VMEM((5, 3 * rows, 2 * cols), f32),
+                pltpu.VMEM((4, rows + 2 * SUB, 2 * cols), f32),
+                pltpu.VMEM((5, rows + 2 * SUB, 2 * cols), f32),
                 pltpu.VMEM((8, 2 * cols), f32),
                 dma((9,)),
                 dma((8,)),
@@ -878,6 +895,15 @@
             land_tiles,
             fold_pair,
         )
+        results = [pltpu.with_memory_space_constraint(result, pltpu.VMEM) for result in results]
+        tracer_new, surface_new, transport_new = pl.pallas_call(
+            write_out,
+            name="write_out",
+            out_shape=tuple(jax.ShapeDtypeStruct(result.shape, f32) for result in results),
+            in_specs=[vmem] * 3,
+            out_specs=(hbm,) * 3,
+            scratch_shapes=[dma((3,))],
+        )(*results)
         return (
             tracer_new.reshape(depth, rows, cols),
             surface_new,

time: 60.9 us -> 59.1 us (0.970)
  local copies, waits for them, and re-layouts: 1.91 us -> 0 us
    unnamed x3 -> x0, local copies, waits for them, and re-layouts: 1.91 us -> none
    pallas_call x0 -> x1, Pallas kernels: none -> 0.74 us  [shards(): pl.pallas_call(write_out, name='write_out', out_shape=tuple((jax.ShapeDty...]
where the time goes in v3:
time: 59.1 us; the launch traced here: 58.9 us
  Pallas kernels  57.6 us (97%)
  between operations  1.29 us (2%)
    pallas_call x1, Pallas kernels, shards(): pl.pallas_call(functools.partial(ocean_kernel, n_lon, n_lat, depth, rows,...  56.9 us

profile of v3, /device:TPU:39, one launch (start us, length us, event | category | flops | bytes accessed | tf_op | source)
XLA Modules:
  0.0 58.9 jit_solution(9866042503807509470)
XLA Ops:
  1.3 56.9 %ocean.1 = (f32[512,128]{1,0:T(8,128)S(1)}, f32[16,128]{1,0:T(8,128)S(1)}, f32[32,128]{1,0:T(8,128)S(1)}) custom-call(f32[512,128]{1,0:T(8,128)} %bitcast.6, f32[1024,128]{1,0:T(8,128)} %bitcast.5, f32[16,128]{1,0:T(8,128)} %surface_hbm.1, f32[32,128]{1,0:T(8,128)} %bitcast.7, s32[16,128]{1,0:T(8,128)} %levels_hbm.1, f32[32]{0:T(128)} %horiz_hbm.1, ...), custom_call_target="tpu_custom_call" | custom-call | tf_op jit(solution)/shard_map/ocean/pallas_call | solution.py:831
  58.2 0.7 %write_out.1 = (f32[512,128]{1,0:T(8,128)}, f32[16,128]{1,0:T(8,128)}, f32[32,128]{1,0:T(8,128)}) custom-call(f32[512,128]{1,0:T(8,128)S(1)} %get-tuple-element.9.a, f32[16,128]{1,0:T(8,128)S(1)} %get-tuple-element.10.b, f32[32,128]{1,0:T(8,128)S(1)} %get-tuple-element.11.c), custom_call_target="tpu_custom_call" | custom-call | tf_op jit(solution)/shard_map/write_out/pallas_call | solution.py:899

commit v4 on v3

--- a/solution.py
+++ b/solution.py
@@ -68,6 +68,7 @@
     coef,
     fold_fix,
     load_sem,
+    hello,
     halo_send,
     halo_recv,
     trac_send,
@@ -133,27 +134,49 @@
     for copy in small:
         copy.start()
     barrier = pltpu.get_barrier_semaphore()
-    peers = [STEP[side] for side in range(8)] + [(2, 0), (-2, 0)]
-    for d_lat, d_lon in peers:
+
+    def signal(sem, d_lat, to):
         pl.semaphore_signal(
-            barrier, inc=1, device_id={"lat": lat_at(d_lat), "lon": lon_at(d_lon)}, device_id_type=MESH
-        )
+            sem, inc=1, device_id={"lat": lat_at(d_lat), "lon": to}, device_id_type=MESH
+        )
+
+    first_lon, last_lon = lon == 0, lon == n_lon - 1
+
+    def signal_side(sem, d_lon):
+        for d_lat in (-1, 0, 1):
+            signal(sem, d_lat, lon_at(d_lon))
+
+    for d_lat in (-2, -1, 1, 2):
+        signal(barrier, d_lat, lon)
+
+    @pl.when(jnp.logical_not(last_lon))
+    def _():
+        signal_side(barrier, 1)
+
+    @pl.when(first_lon)
+    def _():
+        signal_side(barrier, -1)
 
     @pl.when(ring)
     def _():
         @pl.when(keeper)
         def _():
             for g in range(1, n_group):
-                pl.semaphore_signal(barrier, inc=1, device_id={"lon": partner(g)}, device_id_type=MESH)
-
-        @pl.when(has_previous)
-        def _():
-            pl.semaphore_signal(barrier, inc=1, device_id={"lon": lon - onward}, device_id_type=MESH)
-
-        for e in range(1, GROUP):
-            pl.semaphore_signal(
-                barrier, inc=1, device_id={"lon": group + ((me + e) & (GROUP - 1))}, device_id_type=MESH
-            )
+                signal(barrier, 0, partner(g))
+
+        @pl.when(has_previous & jnp.logical_not(rising))
+        def _():
+            signal(barrier, 0, lon - onward)
+
+        @pl.when(has_next & rising)
+        def _():
+            signal(barrier, 0, lon + onward)
+
+        for place in range(1, GROUP):
+
+            @pl.when(place > me)
+            def _(place=place):
+                signal(barrier, 0, group + place)
 
     for copy in large:
         copy.start()
@@ -174,7 +197,7 @@
             side_in[side] = jnp.zeros((8, cols), jnp.float32)
         halo_lat[0] = jnp.zeros((2 * depth, cols), jnp.float32)
 
-    for copy in small:
+    for copy in small[:4]:
         copy.wait()
     dry = 1 - land[0, 0]
     own[pl.ds(3 * rows, rows), :] = (lev[...] * dry).astype(jnp.float32)
@@ -199,8 +222,60 @@
                 slab[pl.ds(at, 1), :] = row if sign == 1 else -row
         slab[pl.ds(block - 8, 1), :] = -own[pl.ds(3 * rows - 1, 1), :]
 
-    pl.semaphore_wait(barrier, len(peers) + jnp.where(ring, GROUP - jnp.where(keeper, 1, 0) + jnp.where(has_next, 1, 0), 0))
-
+    def count(flag, n=1):
+        return jnp.where(flag, n, 0)
+
+    chained = (rising & has_previous) | (jnp.logical_not(rising) & has_next)
+    lower_ring = me + count(jnp.logical_not(keeper)) + count(chained)
+    pl.semaphore_wait(barrier, 4 + count(jnp.logical_not(first_lon), 3) + count(last_lon, 3) + count(ring, lower_ring))
+
+    @pl.when(jnp.logical_not(first_lon))
+    def _():
+        signal_side(hello.at[0], -1)
+
+    @pl.when(last_lon)
+    def _():
+        signal_side(hello.at[0], 1)
+
+    @pl.when(ring)
+    def _():
+        for place in range(GROUP - 1):
+
+            @pl.when(place < me)
+            def _(place=place):
+                signal(hello.at[1], 0, group + place)
+
+        @pl.when(has_previous & rising)
+        def _():
+            signal(hello.at[1], 0, lon - onward)
+
+    def ring_hello():
+        later = GROUP - 1 - me + count(has_next & rising)
+
+        @pl.when(later > 0)
+        def _():
+            pl.semaphore_wait(hello.at[1], later)
+
+    @pl.when(ring & keeper)
+    def _():
+        ring_hello()
+
+    def hold_copy(size):
+        slot = lon >> 2
+        return remote(
+            slab.at[pl.ds(0, size)],
+            hold.at[slot, pl.ds(0, size)],
+            hold_send.at[0],
+            hold_recv.at[slot],
+            {"lon": partner(0)},
+        )
+
+    @pl.when(top)
+    def _():
+        hold_copy(block).start()
+
+    for copy in small[4:]:
+        copy.wait()
     pivot_col = lax.rem(fold[0] + lon * cols, n_lon * cols)
     q = lax.div(pivot_col, cols)
     r = lax.rem(pivot_col, cols)
@@ -224,28 +299,35 @@
         dst = halo.at[0 if side == N else 1] if side in (N, S) else side_in.at[side]
         remote(dst, dst, halo_send.at[side], halo_recv.at[side], {"lon": lon}).wait_recv()
 
-    for side in (E, W):
-        halo_copy(side).start()
+    def halo_side(d_lon, act):
+        act(halo_copy(E if d_lon == 1 else W))
+
+        @pl.when(jnp.logical_not(top))
+        def _():
+            act(halo_copy(NE if d_lon == 1 else NW))
+
+        @pl.when(jnp.logical_not(bottom))
+        def _():
+            act(halo_copy(SE if d_lon == 1 else SW))
+
+    def start(copy):
+        copy.start()
+
+    @pl.when(last_lon)
+    def _():
+        halo_side(1, start)
+
+    @pl.when(jnp.logical_not(first_lon))
+    def _():
+        halo_side(-1, start)
 
     @pl.when(jnp.logical_not(top))
     def _():
-        for side in (N, NE, NW):
-            halo_copy(side).start()
+        halo_copy(N).start()
 
     @pl.when(jnp.logical_not(bottom))
     def _():
-        for side in (S, SE, SW):
-            halo_copy(side).start()
-
-    def hold_copy(size):
-        slot = lon >> 2
-        return remote(
-            slab.at[pl.ds(0, size)],
-            hold.at[slot, pl.ds(0, size)],
-            hold_send.at[0],
-            hold_recv.at[slot],
-            {"lon": partner(0)},
-        )
+        halo_copy(S).start()
 
     def wanted(kind, to):
         low = q - to - 2 + 2 * n_lon
@@ -256,10 +338,6 @@
 
     def lowest(kind, g):
         return wanted(kind, g * GROUP + GROUP - 1) >> 2
-
-    @pl.when(top)
-    def _():
-        hold_copy(block).start()
 
     for copy in large:
         copy.wait()
@@ -331,10 +409,6 @@
             {"lon": lon_at(1 if east else -1)},
         )
 
-    lon_copy(True).start()
-    lon_copy(False).start()
-
-
     def trac_wait(dst, sem):
         remote(dst, dst, trac_send.at[5], sem, {"lon": lon}).wait_recv()
 
@@ -342,6 +416,10 @@
     def _():
         trac_wait(slab.at[pl.ds(0, depth)], trac_recv.at[4])
         hold_copy(depth).start()
+
+    @pl.when(last_lon)
+    def _():
+        lon_copy(True).start()
 
     h_own = own[pl.ds(3 * rows, rows), :]
 
@@ -394,6 +472,18 @@
 
     lax.fori_loop(0, depth, fluxes, 0, unroll=4)
 
+    @pl.when(jnp.logical_not(last_lon))
+    def _():
+        pl.semaphore_wait(hello.at[0], 3 + count(first_lon, 3))
+        halo_side(1, start)
+        lon_copy(True).start()
+
+    @pl.when(first_lon)
+    def _():
+        halo_side(-1, start)
+
+    lon_copy(False).start()
+
     def final_copy(e, size, dst, recv):
         return remote(
             pick.at[e, pl.ds(0, size)], dst, fin_send.at[e], recv, {"lat": n_lat - 1, "lon": group + e}
@@ -599,6 +689,7 @@
 
         @pl.when(role & jnp.logical_not(keeper))
         def _(size=size, target=target):
+            ring_hello()
             chain_wait(0, size)
             chain_wait(1, size)
 
@@ -687,21 +778,29 @@
     coef[2] = fb_step * ((h + north(h)) / (2.0 * depth)) * merid_mask
     coef[3] = (1.0 - drag_rate) * merid_mask
     coef[4] = fb_step * sea
-    fix_decay = pltpu.roll(coef[3], 1, axis=0)[24:32]
+    coef[5] = pltpu.roll(coef[0], 1, axis=1)
+    coef[6] = pltpu.roll(coef[1], 1, axis=1)
+    coef[7] = pltpu.roll(coef[2], 1, axis=0)
+    coef[8] = pltpu.roll(coef[3], 1, axis=0)
+
+    def west(x):
+        return pltpu.roll(x, 1, axis=1)
+
+    def south(x):
+        return pltpu.roll(x, 1, axis=0)
 
     def cycle(i, state):
-        eta, u, v, fix = state
-        v_south = pltpu.roll(v, 1, axis=0)
-        v_south = jnp.concatenate(
-            [v_south[:24], v_south[24:32] + fix, v_south[32:]], axis=0
-        )
-        div = (u - pltpu.roll(u, 1, axis=1)) + (v - v_south)
-        eta = eta - coef[4] * div
+        eta, u, u_west, v, v_south = state
+        eta = eta - coef[4] * ((u - u_west) + (v - v_south))
         u = u * coef[1] - coef[0] * (east(eta) - eta)
         v = v * coef[3] - coef[2] * (north(eta) - eta)
-        return eta, u, v, fix * fix_decay
-
-    eta, u, v, _ = lax.fori_loop(0, SUB, cycle, (ext[0] * sea, ext[1], ext[2], fold_fix[...]))
+        u_west = u_west * coef[6] - coef[5] * (eta - west(eta))
+        v_south = v_south * coef[8] - coef[7] * (eta - south(eta))
+        return eta, u, u_west, v, v_south
+
+    v_south = south(ext[2])
+    v_south = jnp.concatenate([v_south[:24], v_south[24:32] + fold_fix[...], v_south[32:]], axis=0)
+    eta, u, _, v, _ = lax.fori_loop(0, SUB, cycle, (ext[0] * sea, ext[1], west(ext[1]), ext[2], v_south))
     surface_out[...] = eta[low:high, :cols]
     transport_out[pl.ds(0, rows), :] = u[low:high, :cols]
     transport_out[pl.ds(rows, rows), :] = v[low:high, :cols]
@@ -868,9 +967,10 @@
                 pltpu.VMEM((2, depth, cols), f32),
                 pltpu.VMEM((depth, cols), f32),
                 pltpu.VMEM((4, rows + 2 * SUB, 2 * cols), f32),
-                pltpu.VMEM((5, rows + 2 * SUB, 2 * cols), f32),
+                pltpu.VMEM((9, rows + 2 * SUB, 2 * cols), f32),
                 pltpu.VMEM((8, 2 * cols), f32),
                 dma((9,)),
+                pltpu.SemaphoreType.REGULAR((2,)),
                 dma((8,)),
                 dma((8,)),
                 dma((6,)),

time: 59.1 us -> 58 us (0.981)
  Pallas kernels: 57.6 us -> 56.1 us
    pallas_call x1, Pallas kernels: 56.9 us -> 55.4 us  [shards(): pl.pallas_call(functools.partial(ocean_kernel, n_lon, n_lat, depth, rows,...]
where the time goes in v4:
time: 58 us; the launch traced here: 57.4 us
  Pallas kernels  56.1 us (97%)
  between operations  1.29 us (2%)
    pallas_call x1, Pallas kernels, shards(): pl.pallas_call(functools.partial(ocean_kernel, n_lon, n_lat, depth, rows,...  55.4 us

profile of v4, /device:TPU:39, one launch (start us, length us, event | category | flops | bytes accessed | tf_op | source)
XLA Modules:
  0.0 57.4 jit_solution(4254669945843375521)
XLA Ops:
  1.3 55.4 %ocean.1 = (f32[512,128]{1,0:T(8,128)S(1)}, f32[16,128]{1,0:T(8,128)S(1)}, f32[32,128]{1,0:T(8,128)S(1)}) custom-call(f32[512,128]{1,0:T(8,128)} %bitcast.6, f32[1024,128]{1,0:T(8,128)} %bitcast.5, f32[16,128]{1,0:T(8,128)} %surface_hbm.1, f32[32,128]{1,0:T(8,128)} %bitcast.7, s32[16,128]{1,0:T(8,128)} %levels_hbm.1, f32[32]{0:T(128)} %horiz_hbm.1, ...), custom_call_target="tpu_custom_call" | custom-call | tf_op jit(solution)/shard_map/ocean/pallas_call | solution.py:930
  56.7 0.7 %write_out.1 = (f32[512,128]{1,0:T(8,128)}, f32[16,128]{1,0:T(8,128)}, f32[32,128]{1,0:T(8,128)}) custom-call(f32[512,128]{1,0:T(8,128)S(1)} %get-tuple-element.9.a, f32[16,128]{1,0:T(8,128)S(1)} %get-tuple-element.10.b, f32[32,128]{1,0:T(8,128)S(1)} %get-tuple-element.11.c), custom_call_target="tpu_custom_call" | custom-call | tf_op jit(solution)/shard_map/write_out/pallas_call | solution.py:999

commit v5 on v4

--- a/solution.py
+++ b/solution.py
@@ -800,7 +800,7 @@
 
     v_south = south(ext[2])
     v_south = jnp.concatenate([v_south[:24], v_south[24:32] + fold_fix[...], v_south[32:]], axis=0)
-    eta, u, _, v, _ = lax.fori_loop(0, SUB, cycle, (ext[0] * sea, ext[1], west(ext[1]), ext[2], v_south))
+    eta, u, _, v, _ = lax.fori_loop(0, SUB, cycle, (ext[0] * sea, ext[1], west(ext[1]), ext[2], v_south), unroll=4)
     surface_out[...] = eta[low:high, :cols]
     transport_out[pl.ds(0, rows), :] = u[low:high, :cols]
     transport_out[pl.ds(rows, rows), :] = v[low:high, :cols]

time: 58 us -> 57.8 us (level)
  no operation moved by 1% of the time
where the time goes in v5:
time: 57.8 us; the launch traced here: 57.4 us
  Pallas kernels  56.1 us (97%)
  between operations  1.29 us (2%)
    pallas_call x1, Pallas kernels, shards(): pl.pallas_call(functools.partial(ocean_kernel, n_lon, n_lat, depth, rows,...  55.4 us

profile of v5, /device:TPU:39, one launch (start us, length us, event | category | flops | bytes accessed | tf_op | source)
XLA Modules:
  0.0 57.4 jit_solution(309754662536134769)
XLA Ops:
  1.3 55.4 %ocean.1 = (f32[512,128]{1,0:T(8,128)S(1)}, f32[16,128]{1,0:T(8,128)S(1)}, f32[32,128]{1,0:T(8,128)S(1)}) custom-call(f32[512,128]{1,0:T(8,128)} %bitcast.6, f32[1024,128]{1,0:T(8,128)} %bitcast.5, f32[16,128]{1,0:T(8,128)} %surface_hbm.1, f32[32,128]{1,0:T(8,128)} %bitcast.7, s32[16,128]{1,0:T(8,128)} %levels_hbm.1, f32[32]{0:T(128)} %horiz_hbm.1, ...), custom_call_target="tpu_custom_call" | custom-call | tf_op jit(solution)/shard_map/ocean/pallas_call | solution.py:930
  56.7 0.7 %write_out.1 = (f32[512,128]{1,0:T(8,128)}, f32[16,128]{1,0:T(8,128)}, f32[32,128]{1,0:T(8,128)}) custom-call(f32[512,128]{1,0:T(8,128)S(1)} %get-tuple-element.9.a, f32[16,128]{1,0:T(8,128)S(1)} %get-tuple-element.10.b, f32[32,128]{1,0:T(8,128)S(1)} %get-tuple-element.11.c), custom_call_target="tpu_custom_call" | custom-call | tf_op jit(solution)/shard_map/write_out/pallas_call | solution.py:999
